TPU v7x, 1024 devices: a whole 4x4x32 slice. The times are simulated.
1024 devices in a mesh: sub: 256 (over y, z, core), grp: 4 (over x).
Axes of the slice: x: 4, y: 4, z: 32, core: 2. Of those that a mesh axis runs over, the one named last changes fastest.
Arguments:
- dual_ops: float32 [256, 4, 576, 576], P('sub', 'grp'), as said below
- gap_parts: float32 [256, 4, 576, 256], P('sub', 'grp')
- modes: float32 [256, 4, 576, 48], P('sub', 'grp'), may hold values from -0.25 to 0.25
- coarse_rows: float32 [256, 4, 48, 192], P('sub', 'grp'), as said below
- face_live: int32 [256, 4, 6], P('sub', 'grp'), may hold values from 0 to 1, as said below
- contact: int32 [256, 4, 6], P('sub', 'grp'), may hold values from 0 to 1, as said below
Outputs:
- multipliers: float32 [256, 4, 576, 256], P('sub', 'grp')
- direction: float32 [256, 4, 576, 256], P('sub', 'grp')
Inputs may be any that keep to these rules, and one draw needn't show every extreme that they name: Slot k of face_live is 1 only where the subdomain across slot k exists in the geometry (slots 0 and 1 stay within one row of 16 subdomains along sub), and it equals the flag of slot k XOR 1 of that subdomain; face blocks across a shared face list the same points in the same order. `contact`: 1 only where face_live is 1, and equal on both sides of a face. `dual_ops`: each subdomain's block is symmetric positive definite. `coarse_rows`: for each index along sub, the rows of the 4 subdomains stacked in grp order form a symmetric matrix.
All inputs are finite; a program needn't handle non-finite values.
Results may differ from a plain program's by a relative error of at most 0.00012.
Values sent between devices are 32-bit elements; how exact they have to be, the bound alone decides.
No kernel may reach another device: no remote copies, remote signals or barrier semaphores. Data moves between devices by JAX's collectives and lax.ppermute only.
A program may use at most 32 MiB of HBM per device.

v0:
```python
import jax
import jax.numpy as jnp
from jax import lax
from jax.sharding import PartitionSpec as P

SUBROW = 16
ITERS = 2


def shifted(array, axis, by):
    count = lax.axis_size(axis)
    pairs = [(i, i + by) for i in range(count) if 0 <= i + by < count]
    return lax.ppermute(array, axis, pairs)


def across(view):
    gotten = []
    for slot in range(6):
        piece = view[slot ^ 1]
        if slot < 4:
            offset = (1 if slot % 2 == 0 else -1) * (1 if slot < 2 else SUBROW)
            gotten.append(shifted(piece, "sub", offset))
        else:
            offset = 1 if slot == 4 else -1
            gotten.append(shifted(piece, "grp", offset))
    return jnp.stack(gotten)


def assemble(values, live_view, face_rows):
    view = values.reshape(6, face_rows, values.shape[-1])
    return (live_view * (view - across(view))).reshape(values.shape)


def matmul(left, right):
    return jnp.dot(left, right, precision=lax.Precision.HIGHEST, preferred_element_type=jnp.float32)


def body(dual_ops, gap_parts, modes, coarse_rows, face_live, contact):
    operator = dual_ops[0, 0]
    dual_rows = operator.shape[0]
    face_rows = dual_rows // 6
    cases = gap_parts.shape[3]
    live_flags = face_live[0, 0].astype(jnp.float32)
    live_view = live_flags[:, None, None]
    live_rows = jnp.repeat(live_flags, face_rows)[:, None]
    parity = jnp.arange(6) % 2
    upper_rows = jnp.repeat(contact[0, 0] * parity, face_rows)[:, None] > 0
    lower_rows = jnp.repeat(contact[0, 0] * (1 - parity), face_rows)[:, None] > 0
    masked = modes[0, 0] * live_rows
    own_rows = coarse_rows[0, 0]
    gap = assemble(gap_parts[0, 0], live_view, face_rows)
    multipliers = jnp.zeros((dual_rows, cases), jnp.float32)
    direction = multipliers
    for turn in range(ITERS):
        if turn == 0:
            gradient = -gap
        else:
            gradient = assemble(matmul(operator, multipliers), live_view, face_rows) - gap
        coef = matmul(masked.T, gradient)
        coarse = matmul(own_rows, lax.all_gather(coef, "grp", axis=0, tiled=True))
        correction = assemble(matmul(masked, coarse), live_view, face_rows)
        direction = gradient - correction
        norm_terms = jnp.sum(direction * direction, axis=0)
        norm = lax.psum(norm_terms, ("sub", "grp"))
        products = matmul(operator, direction)
        curve_terms = jnp.sum(direction * assemble(products, live_view, face_rows), axis=0)
        curvature = lax.psum(curve_terms, ("sub", "grp"))
        trial = multipliers - (norm / curvature)[None, :] * direction
        multipliers = jnp.where(
            upper_rows,
            jnp.maximum(trial, 0.0),
            jnp.where(lower_rows, jnp.minimum(trial, 0.0), trial),
        )
    return (multipliers[None, None], direction[None, None])


def solution(mesh):
    in_specs = (
        P("sub", "grp", None, None),
        P("sub", "grp", None, None),
        P("sub", "grp", None, None),
        P("sub", "grp", None, None),
        P("sub", "grp", None),
        P("sub", "grp", None),
    )
    out_specs = (P("sub", "grp", None, None), P("sub", "grp", None, None))
    return jax.shard_map(body, mesh=mesh, in_specs=in_specs, out_specs=out_specs, check_vma=False)
```

profile of v0, /device:TPU:1, one launch (start us, length us, event | category | flops | bytes accessed | tf_op | source)
XLA Modules:
  0.0 611.4 jit_solution(15101503540952945535)
XLA Ops:
  0.7 1.3 slice_bitcast_fusion
  2.0 1.3 collective-permute-start.5
  3.3 5.2 collective-permute-start.4
  8.5 1.3 collective-permute-start.3
  9.8 17.0 %collective-permute-start.2 = (f32[96,256]{1,0:T(8,128)S(1)}, f32[96,256]{1,0:T(8,128)}, u32[]{:S(2)}, u32[]{:S(2)}) collective-permute-start(f32[96,256]{1,0:T(8,128)S(1)} %get-tuple-element.43), channel_id=1, source_target_pairs={{0,64},{4,68},{8,72},{12,76},{16,80},{20,84},{24,88},{28,92},{32,9... | collective-permute-start | bytes 294920 | tf_op jit(solution)/shard_map/ppermute | solution.py:13
  26.8 4.9 collective-permute-start
  32.5 7.4 %collective-permute-done = f32[96,256]{1,0:T(8,128)S(1)} collective-permute-done((f32[96,256]{1,0:T(8,128)S(1)}, f32[96,256]{1,0:T(8,128)S(1)}, u32[]{:S(2)}, u32[]{:S(2)}) %collective-permute-start) | collective-permute-done | bytes 98336 | tf_op jit(solution)/shard_map/ppermute | solution.py:13
  40.5 2.0 collective-permute-start.1
  42.6 0.9 bitcast_dynamic-update-slice_fusion.35
  43.5 3.0 collective-permute-done.1
  46.5 0.9 bitcast_dynamic-update-slice_fusion.33
  47.4 0.9 bitcast_dynamic-update-slice_fusion.32
  48.3 0.9 bitcast_dynamic-update-slice_fusion.31
  49.8 9.2 %all_gather.6 = f32[192,256]{1,0:T(8,128)S(1)} all-gather(f32[48,256]{1,0:T(8,128)S(1)} %fusion.30), channel_id=1, replica_groups=mesh['sub'=256,'grp'=4] {'grp'}, dimensions={0}, use_global_device_ids=true | all-gather | bytes 245760 | tf_op jit(solution)/shard_map/all_gather | solution.py:60
  60.4 4.9 collective-permute-start.6
  65.4 1.3 collective-permute-start.11
  66.7 4.0 collective-permute-start.10
  70.7 1.3 collective-permute-start.9
  72.0 19.7 %collective-permute-start.8 = (f32[96,256]{1,0:T(8,128)S(1)}, f32[96,256]{1,0:T(8,128)S(1)}, u32[]{:S(2)}, u32[]{:S(2)}) collective-permute-start(f32[96,256]{1,0:T(8,128)S(1)} %get-tuple-element.37), channel_id=1, source_target_pairs={{0,64},{4,68},{8,72},{12,76},{16,80},{20,84},{24,88},{28,92},{32,9... | collective-permute-start | bytes 294920 | tf_op jit(solution)/shard_map/ppermute | solution.py:13
  91.7 1.9 collective-permute-start.7
  93.6 4.0 collective-permute-done.7
  97.7 2.7 collective-permute-done.9
  100.8 1.6 fusion.6
  102.4 0.8 copy-done.3
  103.2 0.8 fusion.61
  104.0 1.9 collective-permute-start.12
  106.2 1.4 collective-permute-start.17
  107.6 4.0 collective-permute-start.16
  111.6 1.3 collective-permute-start.15
  112.9 18.5 %collective-permute-start.14 = (f32[96,256]{1,0:T(8,128)}, f32[96,256]{1,0:T(8,128)S(1)}, u32[]{:S(2)}, u32[]{:S(2)}) collective-permute-start(f32[96,256]{1,0:T(8,128)} %get-tuple-element.31), channel_id=1, source_target_pairs={{0,64},{4,68},{8,72},{12,76},{16,80},{20,84},{24,88},{28,92},{32,9... | collective-permute-start | bytes 294920 | tf_op jit(solution)/shard_map/ppermute | solution.py:13
  131.5 3.2 collective-permute-start.13
  134.7 0.9 bitcast_dynamic-update-slice_fusion.23
  135.6 2.6 collective-permute-done.13
  138.6 180.3 %all-reduce.1 = (f32[256]{0:T(256)S(1)}, f32[256]{0:T(256)S(1)}) all-reduce(f32[256]{0:T(256)S(1)} %get-tuple-element.5, f32[256]{0:T(256)S(1)} %get-tuple-element.4), channel_id=1, replica_groups=mesh['sub'=256,'grp'=4] {'sub','grp'}, use_global_device_ids=true, to_apply=%region_1.2 | all-reduce | flops 512 | bytes 4096 | tf_op jit(solution)/shard_map/psum | solution.py:64
  319.0 1.8 fusion.9
  320.8 3.3 collective-permute-start.18
  324.1 1.3 collective-permute-start.23
  325.4 4.0 collective-permute-start.22
  329.4 1.3 collective-permute-start.21
  330.7 12.7 %collective-permute-start.20 = (f32[96,256]{1,0:T(8,128)S(1)}, f32[96,256]{1,0:T(8,128)S(1)}, u32[]{:S(2)}, u32[]{:S(2)}) collective-permute-start(f32[96,256]{1,0:T(8,128)S(1)} %get-tuple-element.25), channel_id=1, source_target_pairs={{0,64},{4,68},{8,72},{12,76},{16,80},{20,84},{24,88},{28,92},{32,9... | collective-permute-start | bytes 294920 | tf_op jit(solution)/shard_map/ppermute | solution.py:13
  343.4 2.2 collective-permute-start.19
  345.6 4.1 collective-permute-done.19
  349.7 3.3 collective-permute-done.21
  353.8 9.2 %all_gather.7 = f32[192,256]{1,0:T(8,128)S(1)} all-gather(f32[48,256]{1,0:T(8,128)S(1)} %fusion.45), channel_id=1, replica_groups=mesh['sub'=256,'grp'=4] {'grp'}, dimensions={0}, use_global_device_ids=true | all-gather | bytes 245760 | tf_op jit(solution)/shard_map/all_gather | solution.py:60
  363.7 0.7 fusion.44
  364.5 7.3 %collective-permute-start.24 = (f32[96,256]{1,0:T(8,128)S(1)}, f32[96,256]{1,0:T(8,128)S(1)}, u32[]{:S(2)}, u32[]{:S(2)}) collective-permute-start(f32[96,256]{1,0:T(8,128)S(1)} %get-tuple-element.21), channel_id=1, source_target_pairs={{0,4},{4,8},{8,12},{12,16},{16,20},{20,24},{24,28},{28,32},{32,36}... | collective-permute-start | bytes 294920 | tf_op jit(solution)/shard_map/ppermute | solution.py:13
  371.8 1.3 collective-permute-start.29
  373.1 4.0 collective-permute-start.28
  377.1 1.3 collective-permute-start.27
  378.4 13.7 %collective-permute-start.26 = (f32[96,256]{1,0:T(8,128)S(1)}, f32[96,256]{1,0:T(8,128)S(1)}, u32[]{:S(2)}, u32[]{:S(2)}) collective-permute-start(f32[96,256]{1,0:T(8,128)S(1)} %get-tuple-element.19), channel_id=1, source_target_pairs={{0,64},{4,68},{8,72},{12,76},{16,80},{20,84},{24,88},{28,92},{32,9... | collective-permute-start | bytes 294920 | tf_op jit(solution)/shard_map/ppermute | solution.py:13
  392.1 2.2 collective-permute-start.25
  394.3 4.0 collective-permute-done.25
  398.4 6.4 %collective-permute-done.27 = f32[96,256]{1,0:T(8,128)S(1)} collective-permute-done((f32[96,256]{1,0:T(8,128)S(1)}, f32[96,256]{1,0:T(8,128)S(1)}, u32[]{:S(2)}, u32[]{:S(2)}) %collective-permute-start.27) | collective-permute-done | bytes 98336 | tf_op jit(solution)/shard_map/ppermute | solution.py:13
  405.0 1.6 fusion.12
  406.7 1.9 collective-permute-start.30
  408.6 1.3 collective-permute-start.35
  409.9 4.0 collective-permute-start.34
  413.9 1.3 collective-permute-start.33
  415.2 15.3 %collective-permute-start.32 = (f32[96,256]{1,0:T(8,128)S(1)}, f32[96,256]{1,0:T(8,128)S(1)}, u32[]{:S(2)}, u32[]{:S(2)}) collective-permute-start(f32[96,256]{1,0:T(8,128)S(1)} %get-tuple-element.13), channel_id=1, source_target_pairs={{0,64},{4,68},{8,72},{12,76},{16,80},{20,84},{24,88},{28,92},{32,9... | collective-permute-start | bytes 294920 | tf_op jit(solution)/shard_map/ppermute | solution.py:13
  430.5 3.4 collective-permute-start.31
  433.9 2.5 collective-permute-done.31
  436.5 7.8 %collective-permute-done.33 = f32[96,256]{1,0:T(8,128)S(1)} collective-permute-done((f32[96,256]{1,0:T(8,128)S(1)}, f32[96,256]{1,0:T(8,128)S(1)}, u32[]{:S(2)}, u32[]{:S(2)}) %collective-permute-start.33) | collective-permute-done | bytes 98336 | tf_op jit(solution)/shard_map/ppermute | solution.py:13
  444.6 165.6 %all-reduce = (f32[256]{0:T(256)S(1)}, f32[256]{0:T(256)S(1)}) all-reduce(f32[256]{0:T(256)S(1)} %get-tuple-element.3, f32[256]{0:T(256)S(1)} %get-tuple-element.2), channel_id=1, replica_groups=mesh['sub'=256,'grp'=4] {'sub','grp'}, use_global_device_ids=true, to_apply=%region_5.6 | all-reduce | flops 512 | bytes 4096 | tf_op jit(solution)/shard_map/psum | solution.py:64
  610.3 1.1 fusion.17
  (97 shorter events, 6.6 us)
Async XLA Ops:
  0.6 100.1 %copy-start = (f32[1,1,576,576]{3,2,1,0:T(8,128)S(1)}, f32[1,1,576,576]{3,2,1,0:T(8,128)}, u32[]{:S(2)}) copy-start(f32[1,1,576,576]{3,2,1,0:T(8,128)} %param.6) | copy-start | bytes 3981316
  0.6 48.6 %copy-start.2 = (f32[1,1,576,256]{3,2,1,0:T(8,128)S(1)}, f32[1,1,576,256]{3,2,1,0:T(8,128)}, u32[]{:S(2)}) copy-start(f32[1,1,576,256]{3,2,1,0:T(8,128)} %param.7) | copy-start | bytes 1769476
  0.7 48.6 %copy-start.5 = (f32[1,1,576,48]{2,3,1,0:T(8,128)S(1)}, f32[1,1,576,48]{2,3,1,0:T(8,128)}, u32[]{:S(2)}) copy-start(f32[1,1,576,48]{2,3,1,0:T(8,128)} %param.8) | copy-start | bytes 331780
  2.0 57.0 %copy-start.6 = (f32[1,1,48,192]{3,2,1,0:T(8,128)S(1)}, f32[1,1,48,192]{3,2,1,0:T(8,128)}, u32[]{:S(2)}) copy-start(f32[1,1,48,192]{3,2,1,0:T(8,128)} %param.9) | copy-start | bytes 110596
  2.0 47.2 %collective-permute-start.5 = (f32[96,256]{1,0:T(8,128)S(1)}, f32[96,256]{1,0:T(8,128)S(1)}, u32[]{:S(2)}, u32[]{:S(2)}) collective-permute-start(f32[96,256]{1,0:T(8,128)S(1)} %get-tuple-element.40), channel_id=1, source_target_pairs={{1,0},{2,1},{3,2},{5,4},{6,5},{7,6},{9,8},{10,9},{11,10},{13,12},{... | collective-permute-start | bytes 294920 | tf_op jit(solution)/shard_map/ppermute | solution.py:13
  3.3 45.0 %collective-permute-start.4 = (f32[96,256]{1,0:T(8,128)S(1)}, f32[96,256]{1,0:T(8,128)}, u32[]{:S(2)}, u32[]{:S(2)}) collective-permute-start(f32[96,256]{1,0:T(8,128)S(1)} %get-tuple-element.41), channel_id=1, source_target_pairs={{0,1},{1,2},{2,3},{4,5},{5,6},{6,7},{8,9},{9,10},{10,11},{12,13},{... | collective-permute-start | bytes 294920 | tf_op jit(solution)/shard_map/ppermute | solution.py:13
  8.5 38.9 %collective-permute-start.3 = (f32[96,256]{1,0:T(8,128)S(1)}, f32[96,256]{1,0:T(8,128)}, u32[]{:S(2)}, u32[]{:S(2)}) collective-permute-start(f32[96,256]{1,0:T(8,128)S(1)} %get-tuple-element.42), channel_id=1, source_target_pairs={{64,0},{68,4},{72,8},{76,12},{80,16},{84,20},{88,24},{92,28},{96,3... | collective-permute-start | bytes 294920 | tf_op jit(solution)/shard_map/ppermute | solution.py:13
  9.8 36.7 %collective-permute-start.2 = (f32[96,256]{1,0:T(8,128)S(1)}, f32[96,256]{1,0:T(8,128)}, u32[]{:S(2)}, u32[]{:S(2)}) collective-permute-start(f32[96,256]{1,0:T(8,128)S(1)} %get-tuple-element.43), channel_id=1, source_target_pairs={{0,64},{4,68},{8,72},{12,76},{16,80},{20,84},{24,88},{28,92},{32,9... | collective-permute-start | bytes 294920 | tf_op jit(solution)/shard_map/ppermute | solution.py:13
  26.8 13.1 %collective-permute-start = (f32[96,256]{1,0:T(8,128)S(1)}, f32[96,256]{1,0:T(8,128)S(1)}, u32[]{:S(2)}, u32[]{:S(2)}) collective-permute-start(f32[96,256]{1,0:T(8,128)S(1)} %get-tuple-element.45), channel_id=1, source_target_pairs={{0,4},{4,8},{8,12},{12,16},{16,20},{20,24},{24,28},{28,32},{32,36}... | collective-permute-start | bytes 294920 | tf_op jit(solution)/shard_map/ppermute | solution.py:13
  39.9 0.6 copy-start.7
  40.5 5.9 collective-permute-start.1
  60.4 31.2 %collective-permute-start.6 = (f32[96,256]{1,0:T(8,128)S(1)}, f32[96,256]{1,0:T(8,128)S(1)}, u32[]{:S(2)}, u32[]{:S(2)}) collective-permute-start(f32[96,256]{1,0:T(8,128)S(1)} %get-tuple-element.39), channel_id=1, source_target_pairs={{0,4},{4,8},{8,12},{12,16},{16,20},{20,24},{24,28},{28,32},{32,36}... | collective-permute-start | bytes 294920 | tf_op jit(solution)/shard_map/ppermute | solution.py:13
  65.4 35.0 %collective-permute-start.11 = (f32[96,256]{1,0:T(8,128)S(1)}, f32[96,256]{1,0:T(8,128)S(1)}, u32[]{:S(2)}, u32[]{:S(2)}) collective-permute-start(f32[96,256]{1,0:T(8,128)S(1)} %get-tuple-element.34), channel_id=1, source_target_pairs={{1,0},{2,1},{3,2},{5,4},{6,5},{7,6},{9,8},{10,9},{11,10},{13,12},{... | collective-permute-start | bytes 294920 | tf_op jit(solution)/shard_map/ppermute | solution.py:13
  66.7 33.7 %collective-permute-start.10 = (f32[96,256]{1,0:T(8,128)S(1)}, f32[96,256]{1,0:T(8,128)S(1)}, u32[]{:S(2)}, u32[]{:S(2)}) collective-permute-start(f32[96,256]{1,0:T(8,128)S(1)} %get-tuple-element.35), channel_id=1, source_target_pairs={{0,1},{1,2},{2,3},{4,5},{5,6},{6,7},{8,9},{9,10},{10,11},{12,13},{... | collective-permute-start | bytes 294920 | tf_op jit(solution)/shard_map/ppermute | solution.py:13
  70.7 29.7 %collective-permute-start.9 = (f32[96,256]{1,0:T(8,128)S(1)}, f32[96,256]{1,0:T(8,128)S(1)}, u32[]{:S(2)}, u32[]{:S(2)}) collective-permute-start(f32[96,256]{1,0:T(8,128)S(1)} %get-tuple-element.36), channel_id=1, source_target_pairs={{64,0},{68,4},{72,8},{76,12},{80,16},{84,20},{88,24},{92,28},{96,3... | collective-permute-start | bytes 294920 | tf_op jit(solution)/shard_map/ppermute | solution.py:13
  72.0 25.6 %collective-permute-start.8 = (f32[96,256]{1,0:T(8,128)S(1)}, f32[96,256]{1,0:T(8,128)S(1)}, u32[]{:S(2)}, u32[]{:S(2)}) collective-permute-start(f32[96,256]{1,0:T(8,128)S(1)} %get-tuple-element.37), channel_id=1, source_target_pairs={{0,64},{4,68},{8,72},{12,76},{16,80},{20,84},{24,88},{28,92},{32,9... | collective-permute-start | bytes 294920 | tf_op jit(solution)/shard_map/ppermute | solution.py:13
  91.7 5.9 collective-permute-start.7
  100.7 5.1 copy-start.8
  102.4 0.8 copy-start.3
  104.0 27.5 %collective-permute-start.12 = (f32[96,256]{1,0:T(8,128)}, f32[96,256]{1,0:T(8,128)}, u32[]{:S(2)}, u32[]{:S(2)}) collective-permute-start(f32[96,256]{1,0:T(8,128)} %get-tuple-element.33), channel_id=1, source_target_pairs={{0,4},{4,8},{8,12},{12,16},{16,20},{20,24},{24,28},{28,32},{32,36}... | collective-permute-start | bytes 294920 | tf_op jit(solution)/shard_map/ppermute | solution.py:13
  106.2 32.2 %copy-start.4 = (f32[576,256]{1,0:T(8,128)S(1)}, f32[576,256]{1,0:T(8,128)}, u32[]{:S(2)}) copy-start(f32[576,256]{1,0:T(8,128)} %copy-done.3) | copy-start | bytes 1769476
  106.2 32.1 %collective-permute-start.17 = (f32[96,256]{1,0:T(8,128)S(1)}, f32[96,256]{1,0:T(8,128)S(1)}, u32[]{:S(2)}, u32[]{:S(2)}) collective-permute-start(f32[96,256]{1,0:T(8,128)S(1)} %get-tuple-element.28), channel_id=1, source_target_pairs={{1,0},{2,1},{3,2},{5,4},{6,5},{7,6},{9,8},{10,9},{11,10},{13,12},{... | collective-permute-start | bytes 294920 | tf_op jit(solution)/shard_map/ppermute | solution.py:13
  107.6 30.7 %collective-permute-start.16 = (f32[96,256]{1,0:T(8,128)}, f32[96,256]{1,0:T(8,128)S(1)}, u32[]{:S(2)}, u32[]{:S(2)}) collective-permute-start(f32[96,256]{1,0:T(8,128)} %get-tuple-element.29), channel_id=1, source_target_pairs={{0,1},{1,2},{2,3},{4,5},{5,6},{6,7},{8,9},{9,10},{10,11},{12,13},{... | collective-permute-start | bytes 294920 | tf_op jit(solution)/shard_map/ppermute | solution.py:13
  111.6 26.7 %collective-permute-start.15 = (f32[96,256]{1,0:T(8,128)}, f32[96,256]{1,0:T(8,128)S(1)}, u32[]{:S(2)}, u32[]{:S(2)}) collective-permute-start(f32[96,256]{1,0:T(8,128)} %get-tuple-element.30), channel_id=1, source_target_pairs={{64,0},{68,4},{72,8},{76,12},{80,16},{84,20},{88,24},{92,28},{96,3... | collective-permute-start | bytes 294920 | tf_op jit(solution)/shard_map/ppermute | solution.py:13
  112.9 25.3 %collective-permute-start.14 = (f32[96,256]{1,0:T(8,128)}, f32[96,256]{1,0:T(8,128)S(1)}, u32[]{:S(2)}, u32[]{:S(2)}) collective-permute-start(f32[96,256]{1,0:T(8,128)} %get-tuple-element.31), channel_id=1, source_target_pairs={{0,64},{4,68},{8,72},{12,76},{16,80},{20,84},{24,88},{28,92},{32,9... | collective-permute-start | bytes 294920 | tf_op jit(solution)/shard_map/ppermute | solution.py:13
  131.5 6.8 %collective-permute-start.13 = (f32[96,256]{1,0:T(8,128)}, f32[96,256]{1,0:T(8,128)S(1)}, u32[]{:S(2)}, u32[]{:S(2)}) collective-permute-start(f32[96,256]{1,0:T(8,128)} %get-tuple-element.32), channel_id=1, source_target_pairs={{4,0},{8,4},{12,8},{16,12},{20,16},{24,20},{28,24},{32,28},{36,32}... | collective-permute-start | bytes 294920 | tf_op jit(solution)/shard_map/ppermute | solution.py:13
  320.8 22.6 %collective-permute-start.18 = (f32[96,256]{1,0:T(8,128)S(1)}, f32[96,256]{1,0:T(8,128)S(1)}, u32[]{:S(2)}, u32[]{:S(2)}) collective-permute-start(f32[96,256]{1,0:T(8,128)S(1)} %get-tuple-element.27), channel_id=1, source_target_pairs={{0,4},{4,8},{8,12},{12,16},{16,20},{20,24},{24,28},{28,32},{32,36}... | collective-permute-start | bytes 294920 | tf_op jit(solution)/shard_map/ppermute | solution.py:13
  324.1 28.9 %collective-permute-start.23 = (f32[96,256]{1,0:T(8,128)S(1)}, f32[96,256]{1,0:T(8,128)S(1)}, u32[]{:S(2)}, u32[]{:S(2)}) collective-permute-start(f32[96,256]{1,0:T(8,128)S(1)} %get-tuple-element.22), channel_id=1, source_target_pairs={{1,0},{2,1},{3,2},{5,4},{6,5},{7,6},{9,8},{10,9},{11,10},{13,12},{... | collective-permute-start | bytes 294920 | tf_op jit(solution)/shard_map/ppermute | solution.py:13
  325.4 27.6 %collective-permute-start.22 = (f32[96,256]{1,0:T(8,128)S(1)}, f32[96,256]{1,0:T(8,128)S(1)}, u32[]{:S(2)}, u32[]{:S(2)}) collective-permute-start(f32[96,256]{1,0:T(8,128)S(1)} %get-tuple-element.23), channel_id=1, source_target_pairs={{0,1},{1,2},{2,3},{4,5},{5,6},{6,7},{8,9},{9,10},{10,11},{12,13},{... | collective-permute-start | bytes 294920 | tf_op jit(solution)/shard_map/ppermute | solution.py:13
  329.4 23.6 %collective-permute-start.21 = (f32[96,256]{1,0:T(8,128)S(1)}, f32[96,256]{1,0:T(8,128)S(1)}, u32[]{:S(2)}, u32[]{:S(2)}) collective-permute-start(f32[96,256]{1,0:T(8,128)S(1)} %get-tuple-element.24), channel_id=1, source_target_pairs={{64,0},{68,4},{72,8},{76,12},{80,16},{84,20},{88,24},{92,28},{96,3... | collective-permute-start | bytes 294920 | tf_op jit(solution)/shard_map/ppermute | solution.py:13
  330.7 19.0 %collective-permute-start.20 = (f32[96,256]{1,0:T(8,128)S(1)}, f32[96,256]{1,0:T(8,128)S(1)}, u32[]{:S(2)}, u32[]{:S(2)}) collective-permute-start(f32[96,256]{1,0:T(8,128)S(1)} %get-tuple-element.25), channel_id=1, source_target_pairs={{0,64},{4,68},{8,72},{12,76},{16,80},{20,84},{24,88},{28,92},{32,9... | collective-permute-start | bytes 294920 | tf_op jit(solution)/shard_map/ppermute | solution.py:13
  343.4 6.3 %collective-permute-start.19 = (f32[96,256]{1,0:T(8,128)S(1)}, f32[96,256]{1,0:T(8,128)S(1)}, u32[]{:S(2)}, u32[]{:S(2)}) collective-permute-start(f32[96,256]{1,0:T(8,128)S(1)} %get-tuple-element.26), channel_id=1, source_target_pairs={{4,0},{8,4},{12,8},{16,12},{20,16},{24,20},{28,24},{32,28},{36,32}... | collective-permute-start | bytes 294920 | tf_op jit(solution)/shard_map/ppermute | solution.py:13
  364.5 27.6 %collective-permute-start.24 = (f32[96,256]{1,0:T(8,128)S(1)}, f32[96,256]{1,0:T(8,128)S(1)}, u32[]{:S(2)}, u32[]{:S(2)}) collective-permute-start(f32[96,256]{1,0:T(8,128)S(1)} %get-tuple-element.21), channel_id=1, source_target_pairs={{0,4},{4,8},{8,12},{12,16},{16,20},{20,24},{24,28},{28,32},{32,36}... | collective-permute-start | bytes 294920 | tf_op jit(solution)/shard_map/ppermute | solution.py:13
  371.8 33.0 %collective-permute-start.29 = (f32[96,256]{1,0:T(8,128)S(1)}, f32[96,256]{1,0:T(8,128)S(1)}, u32[]{:S(2)}, u32[]{:S(2)}) collective-permute-start(f32[96,256]{1,0:T(8,128)S(1)} %get-tuple-element.16), channel_id=1, source_target_pairs={{1,0},{2,1},{3,2},{5,4},{6,5},{7,6},{9,8},{10,9},{11,10},{13,12},{... | collective-permute-start | bytes 294920 | tf_op jit(solution)/shard_map/ppermute | solution.py:13
  373.1 31.7 %collective-permute-start.28 = (f32[96,256]{1,0:T(8,128)S(1)}, f32[96,256]{1,0:T(8,128)S(1)}, u32[]{:S(2)}, u32[]{:S(2)}) collective-permute-start(f32[96,256]{1,0:T(8,128)S(1)} %get-tuple-element.17), channel_id=1, source_target_pairs={{0,1},{1,2},{2,3},{4,5},{5,6},{6,7},{8,9},{9,10},{10,11},{12,13},{... | collective-permute-start | bytes 294920 | tf_op jit(solution)/shard_map/ppermute | solution.py:13
  377.1 27.7 %collective-permute-start.27 = (f32[96,256]{1,0:T(8,128)S(1)}, f32[96,256]{1,0:T(8,128)S(1)}, u32[]{:S(2)}, u32[]{:S(2)}) collective-permute-start(f32[96,256]{1,0:T(8,128)S(1)} %get-tuple-element.18), channel_id=1, source_target_pairs={{64,0},{68,4},{72,8},{76,12},{80,16},{84,20},{88,24},{92,28},{96,3... | collective-permute-start | bytes 294920 | tf_op jit(solution)/shard_map/ppermute | solution.py:13
  378.4 19.9 %collective-permute-start.26 = (f32[96,256]{1,0:T(8,128)S(1)}, f32[96,256]{1,0:T(8,128)S(1)}, u32[]{:S(2)}, u32[]{:S(2)}) collective-permute-start(f32[96,256]{1,0:T(8,128)S(1)} %get-tuple-element.19), channel_id=1, source_target_pairs={{0,64},{4,68},{8,72},{12,76},{16,80},{20,84},{24,88},{28,92},{32,9... | collective-permute-start | bytes 294920 | tf_op jit(solution)/shard_map/ppermute | solution.py:13
  392.1 6.2 %collective-permute-start.25 = (f32[96,256]{1,0:T(8,128)S(1)}, f32[96,256]{1,0:T(8,128)S(1)}, u32[]{:S(2)}, u32[]{:S(2)}) collective-permute-start(f32[96,256]{1,0:T(8,128)S(1)} %get-tuple-element.20), channel_id=1, source_target_pairs={{4,0},{8,4},{12,8},{16,12},{20,16},{24,20},{28,24},{32,28},{36,32}... | collective-permute-start | bytes 294920 | tf_op jit(solution)/shard_map/ppermute | solution.py:13
  405.0 205.3 %copy-start.1 = (f32[576,256]{1,0:T(8,128)}, f32[576,256]{1,0:T(8,128)S(1)}, u32[]{:S(2)}) copy-start(f32[576,256]{1,0:T(8,128)S(1)} %fusion.22) | copy-start | bytes 1769476
  406.7 23.8 %collective-permute-start.30 = (f32[96,256]{1,0:T(8,128)S(1)}, f32[96,256]{1,0:T(8,128)S(1)}, u32[]{:S(2)}, u32[]{:S(2)}) collective-permute-start(f32[96,256]{1,0:T(8,128)S(1)} %get-tuple-element.15), channel_id=1, source_target_pairs={{0,4},{4,8},{8,12},{12,16},{16,20},{20,24},{24,28},{28,32},{32,36}... | collective-permute-start | bytes 294920 | tf_op jit(solution)/shard_map/ppermute | solution.py:13
  408.6 35.8 %collective-permute-start.35 = (f32[96,256]{1,0:T(8,128)S(1)}, f32[96,256]{1,0:T(8,128)S(1)}, u32[]{:S(2)}, u32[]{:S(2)}) collective-permute-start(f32[96,256]{1,0:T(8,128)S(1)} %get-tuple-element.10), channel_id=1, source_target_pairs={{1,0},{2,1},{3,2},{5,4},{6,5},{7,6},{9,8},{10,9},{11,10},{13,12},{... | collective-permute-start | bytes 294920 | tf_op jit(solution)/shard_map/ppermute | solution.py:13
  409.9 34.4 %collective-permute-start.34 = (f32[96,256]{1,0:T(8,128)S(1)}, f32[96,256]{1,0:T(8,128)S(1)}, u32[]{:S(2)}, u32[]{:S(2)}) collective-permute-start(f32[96,256]{1,0:T(8,128)S(1)} %get-tuple-element.11), channel_id=1, source_target_pairs={{0,1},{1,2},{2,3},{4,5},{5,6},{6,7},{8,9},{9,10},{10,11},{12,13},{... | collective-permute-start | bytes 294920 | tf_op jit(solution)/shard_map/ppermute | solution.py:13
  413.9 30.4 %collective-permute-start.33 = (f32[96,256]{1,0:T(8,128)S(1)}, f32[96,256]{1,0:T(8,128)S(1)}, u32[]{:S(2)}, u32[]{:S(2)}) collective-permute-start(f32[96,256]{1,0:T(8,128)S(1)} %get-tuple-element.12), channel_id=1, source_target_pairs={{64,0},{68,4},{72,8},{76,12},{80,16},{84,20},{88,24},{92,28},{96,3... | collective-permute-start | bytes 294920 | tf_op jit(solution)/shard_map/ppermute | solution.py:13
  415.2 21.3 %collective-permute-start.32 = (f32[96,256]{1,0:T(8,128)S(1)}, f32[96,256]{1,0:T(8,128)S(1)}, u32[]{:S(2)}, u32[]{:S(2)}) collective-permute-start(f32[96,256]{1,0:T(8,128)S(1)} %get-tuple-element.13), channel_id=1, source_target_pairs={{0,64},{4,68},{8,72},{12,76},{16,80},{20,84},{24,88},{28,92},{32,9... | collective-permute-start | bytes 294920 | tf_op jit(solution)/shard_map/ppermute | solution.py:13
  430.5 5.9 collective-permute-start.31
where the time goes:
time: 613 us; the launch traced here: 611 us
  blocking collectives  364 us (59%)
  starting transfers between devices  177 us (29%)
  waiting for transfers between devices  47.9 us (8%)
  local copies, waits for them, and re-layouts  9.03 us (1%)
  matrix products  8.6 us (1%)
    psum x2, blocking collectives, body(): norm = lax.psum(norm_terms, ('sub', 'grp'))  346 us
    ppermute x36, starting transfers between devices, shifted(): return lax.ppermute(array, axis, pairs)  177 us
    ppermute x36, waiting for transfers between devices, shifted(): return lax.ppermute(array, axis, pairs)  47.9 us
    all_gather x2, blocking collectives, body(): coarse = matmul(own_rows, lax.all_gather(coef, 'grp', axis=0, tiled=True))  18.5 us
  transfers between devices with their start and end apart: 36, of which 11 were waited for; matrix products, arithmetic and copies ran while one was open for 1% of the time, Pallas kernels for 0%

commit v1 on v0

v1 whole, which is shorter than its diff:
```python
import jax
import jax.numpy as jnp
from jax import lax
from jax.sharding import PartitionSpec as P

SUBROW = 16
SOURCES = (("sub", -1), ("sub", 1), ("sub", -SUBROW), ("sub", SUBROW), ("grp", -1), ("grp", 1))
ORDER = (2, 3, 0, 1, 4, 5)


def shifted(array, axis, by):
    count = lax.axis_size(axis)
    pairs = [(i, i + by) for i in range(count) if 0 <= i + by < count]
    return lax.ppermute(array, axis, pairs)


def fetch(piece, slot):
    axis, offset = SOURCES[slot]
    return shifted(piece, axis, -offset)


def across(view):
    gotten = [None] * 6
    for slot in ORDER:
        gotten[slot] = fetch(view[slot ^ 1], slot)
    return jnp.stack(gotten)


def matmul(left, right):
    return jnp.dot(left, right, precision=lax.Precision.HIGHEST, preferred_element_type=jnp.float32)


def clamp(values, upper, lower):
    return jnp.where(upper, jnp.maximum(values, 0.0), jnp.where(lower, jnp.minimum(values, 0.0), values))


def total(terms):
    return lax.psum(terms, ("sub", "grp"))


def body(dual_ops, gap_parts, modes, coarse_rows, face_live, contact):
    operator = dual_ops[0, 0]
    dual_rows = operator.shape[0]
    face_rows = dual_rows // 6
    cases = gap_parts.shape[3]
    kinds = modes.shape[3]
    live_flags = face_live[0, 0].astype(jnp.float32)
    live_view = live_flags[:, None, None]
    parity = jnp.arange(6) % 2
    upper = (contact[0, 0] * parity)[:, None, None] > 0
    lower = (contact[0, 0] * (1 - parity))[:, None, None] > 0
    masked = modes[0, 0].reshape(6, face_rows, kinds) * live_view
    own_rows = coarse_rows[0, 0]

    parts = gap_parts[0, 0].reshape(6, face_rows, cases)
    parts_across = across(parts)
    masked_across = across(masked)
    all_rows = jnp.concatenate([own_rows, fetch(own_rows, 4), fetch(own_rows, 5)])

    masked_flat = masked.reshape(dual_rows, kinds)
    pairs = jnp.concatenate([masked, -masked_across], axis=2)

    def projected(values):
        coef = matmul(masked_flat.T, values.reshape(dual_rows, cases))
        coarse = matmul(all_rows, lax.all_gather(coef, "grp", axis=0, tiled=True))
        own = coarse[:kinds]
        near = [None] * 4
        for slot in ORDER[:4]:
            near[slot] = fetch(own, slot)
        near += [coarse[kinds:2 * kinds], coarse[2 * kinds:]]
        stacked = jnp.stack([jnp.concatenate([own, other]) for other in near])
        correction = jnp.einsum(
            "kij,kjl->kil", pairs, stacked, precision=lax.Precision.HIGHEST, preferred_element_type=jnp.float32
        )
        return values - correction

    def apply_local(values):
        return matmul(operator, values.reshape(dual_rows, cases)).reshape(6, face_rows, cases)

    first = projected(live_view * (parts_across - parts))
    push = clamp(-first, upper, lower)
    pushed = apply_local(push)
    first_image = apply_local(first)
    change = projected(live_view * (pushed - across(pushed)))
    change_image = apply_local(change)

    def inner(left, right):
        return jnp.sum(left * right, axis=(0, 1))

    sums = total(jnp.stack([
        inner(first, first), inner(first, first_image), inner(first, change),
        inner(change, change), inner(change, first_image), inner(change, change_image),
    ]))
    step = sums[0] / (2.0 * sums[1])
    norm = sums[0] + step * (2.0 * sums[2] + step * sums[3])
    curvature = 2.0 * (sums[1] + step * (2.0 * sums[4] + step * sums[5]))
    direction = first + step * change
    multipliers = clamp(step * push - (norm / curvature) * direction, upper, lower)
    shape = (1, 1, dual_rows, cases)
    return (multipliers.reshape(shape), direction.reshape(shape))


def solution(mesh):
    in_specs = (
        P("sub", "grp", None, None),
        P("sub", "grp", None, None),
        P("sub", "grp", None, None),
        P("sub", "grp", None, None),
        P("sub", "grp", None),
        P("sub", "grp", None),
    )
    out_specs = (P("sub", "grp", None, None), P("sub", "grp", None, None))
    return jax.shard_map(body, mesh=mesh, in_specs=in_specs, out_specs=out_specs, check_vma=False)
```

time: 613 us -> 412 us (0.67)
  blocking collectives: 364 us -> 187 us
  starting transfers between devices: 177 us -> 112 us
  waiting for transfers between devices: 47.9 us -> 92.2 us
    psum x2 -> x1, blocking collectives: 346 us -> 167 us  [total(): return lax.psum(terms, ('sub', 'grp'))]
    ppermute x36 -> x28, starting transfers between devices: 177 us -> 112 us  [shifted(): return lax.ppermute(array, axis, pairs)]
    ppermute x36 -> x28, waiting for transfers between devices: 47.9 us -> 92.2 us  [shifted(): return lax.ppermute(array, axis, pairs)]
  transfers between devices with their start and end apart: 36 -> 28, of which waited for: 11 -> 10; matrix products, arithmetic and copies ran while one was open for 1% -> 2% of each run, Pallas kernels for 0% -> 0%
where the time goes in v1:
time: 412 us; the launch traced here: 411 us
  blocking collectives  187 us (45%)
  starting transfers between devices  112 us (27%)
  waiting for transfers between devices  92.2 us (22%)
  matrix products  7.98 us (2%)
  local copies, waits for them, and re-layouts  7.5 us (2%)
    psum x1, blocking collectives, total(): return lax.psum(terms, ('sub', 'grp'))  167 us
    ppermute x28, starting transfers between devices, shifted(): return lax.ppermute(array, axis, pairs)  112 us
    ppermute x28, waiting for transfers between devices, shifted(): return lax.ppermute(array, axis, pairs)  92.2 us
    all_gather x2, blocking collectives, projected(): coarse = matmul(all_rows, lax.all_gather(coef, 'grp', axis=0, tiled=True))  20.8 us
  transfers between devices with their start and end apart: 28, of which 10 were waited for; matrix products, arithmetic and copies ran while one was open for 2% of the time, Pallas kernels for 0%

profile of v1, /device:TPU:1, one launch (start us, length us, event | category | flops | bytes accessed | tf_op | source)
XLA Modules:
  0.0 410.9 jit_solution(10516862953986159538)
XLA Ops:
  0.7 4.1 collective-permute-start.12
  4.7 1.3 collective-permute-start.13
  6.0 1.8 slice_bitcast_fusion.2
  7.8 4.4 %collective-permute-start = (f32[96,256]{1,0:T(8,128)S(1)}, f32[96,256]{1,0:T(8,128)}, u32[]{:S(2)}, u32[]{:S(2)}) collective-permute-start(f32[96,256]{1,0:T(8,128)S(1)} %get-tuple-element.21), channel_id=1, source_target_pairs={{0,4},{4,8},{8,12},{12,16},{16,20},{20,24},{24,28},{28,32},{32,36}... | collective-permute-start | bytes 294920 | tf_op jit(solution)/shard_map/ppermute | solution.py:14
  12.2 10.9 %collective-permute-start.1 = (f32[96,256]{1,0:T(8,128)S(1)}, f32[96,256]{1,0:T(8,128)}, u32[]{:S(2)}, u32[]{:S(2)}) collective-permute-start(f32[96,256]{1,0:T(8,128)S(1)} %get-tuple-element.20), channel_id=1, source_target_pairs={{4,0},{8,4},{12,8},{16,12},{20,16},{24,20},{28,24},{32,28},{36,32}... | collective-permute-start | bytes 294920 | tf_op jit(solution)/shard_map/ppermute | solution.py:14
  23.1 0.7 convert_bitcast_fusion
  23.8 1.0 copy.9
  24.9 0.1 broadcast_multiply_fusion
  25.0 2.1 collective-permute-start.6
  27.1 0.1 mul.170
  27.2 0.1 mul.171
  27.2 1.0 collective-permute-done.6
  28.3 2.1 collective-permute-start.7
  30.3 3.9 collective-permute-done.7
  34.2 8.2 %collective-permute-start.8 = (f32[96,48]{1,0:T(8,128)S(1)}, f32[96,48]{1,0:T(8,128)S(1)}, u32[]{:S(2)}, u32[]{:S(2)}) collective-permute-start(f32[96,48]{1,0:T(8,128)S(1)} %get-tuple-element.25), channel_id=1, source_target_pairs={{0,64},{4,68},{8,72},{12,76},{16,80},{20,84},{24,88},{28,92},{32,9... | collective-permute-start | bytes 55304 | tf_op jit(solution)/shard_map/ppermute | solution.py:14
  42.4 1.1 collective-permute-done.8
  43.6 1.3 collective-permute-start.9
  44.9 26.7 %collective-permute-done.9 = f32[96,48]{1,0:T(8,128)S(1)} collective-permute-done((f32[96,48]{1,0:T(8,128)S(1)}, f32[96,48]{1,0:T(8,128)S(1)}, u32[]{:S(2)}, u32[]{:S(2)}) %collective-permute-start.9) | collective-permute-done | bytes 18464 | tf_op jit(solution)/shard_map/ppermute | solution.py:14
  71.5 4.4 %collective-permute-start.10 = (f32[96,48]{1,0:T(8,128)S(1)}, f32[96,48]{1,0:T(8,128)S(1)}, u32[]{:S(2)}, u32[]{:S(2)}) collective-permute-start(f32[96,48]{1,0:T(8,128)S(1)} %get-tuple-element.23), channel_id=1, source_target_pairs={{0,1},{1,2},{2,3},{4,5},{5,6},{6,7},{8,9},{9,10},{10,11},{12,13},{... | collective-permute-start | bytes 55304 | tf_op jit(solution)/shard_map/ppermute | solution.py:14
  76.0 1.1 collective-permute-done.10
  77.1 12.7 %collective-permute-start.2 = (f32[96,256]{1,0:T(8,128)S(1)}, f32[96,256]{1,0:T(8,128)S(1)}, u32[]{:S(2)}, u32[]{:S(2)}) collective-permute-start(f32[96,256]{1,0:T(8,128)S(1)} %get-tuple-element.19), channel_id=1, source_target_pairs={{0,64},{4,68},{8,72},{12,76},{16,80},{20,84},{24,88},{28,92},{32,9... | collective-permute-start | bytes 294920 | tf_op jit(solution)/shard_map/ppermute | solution.py:14
  89.9 1.3 collective-permute-start.3
  91.2 0.9 bitcast_dynamic-update-slice_fusion.11
  92.1 3.7 collective-permute-start.4
  95.8 0.9 bitcast_dynamic-update-slice_fusion.10
  96.7 1.3 collective-permute-start.5
  98.0 15.7 %collective-permute-done.3 = f32[96,256]{1,0:T(8,128)S(1)} collective-permute-done((f32[96,256]{1,0:T(8,128)S(1)}, f32[96,256]{1,0:T(8,128)S(1)}, u32[]{:S(2)}, u32[]{:S(2)}) %collective-permute-start.3) | collective-permute-done | bytes 98336 | tf_op jit(solution)/shard_map/ppermute | solution.py:14
  113.7 1.3 collective-permute-start.11
  115.1 0.6 fusion.9
  115.7 11.5 %all_gather.6 = f32[192,256]{1,0:T(8,128)S(1)} all-gather(f32[48,256]{1,0:T(8,128)S(1)} %fusion.9), channel_id=1, replica_groups=mesh['sub'=256,'grp'=4] {'grp'}, dimensions={0}, use_global_device_ids=true | all-gather | bytes 245760 | tf_op jit(solution)/shard_map/all_gather | solution.py:65
  127.2 0.3 fusion.17
  127.5 3.2 collective-permute-start.14
  130.8 3.1 collective-permute-start.15
  133.9 10.7 %collective-permute-start.16 = (f32[48,256]{1,0:T(8,128)S(1)}, f32[48,256]{1,0:T(8,128)S(1)}, u32[]{:S(2)}, u32[]{:S(2)}) collective-permute-start(f32[48,256]{1,0:T(8,128)S(1)} %get-tuple-element.31), channel_id=1, source_target_pairs={{0,64},{4,68},{8,72},{12,76},{16,80},{20,84},{24,88},{28,92},{32,9... | collective-permute-start | bytes 147464 | tf_op jit(solution)/shard_map/ppermute | solution.py:14
  144.6 1.3 collective-permute-start.17
  146.0 2.4 collective-permute-done.16
  148.4 10.5 %collective-permute-done.17 = f32[48,256]{1,0:T(8,128)S(1)} collective-permute-done((f32[48,256]{1,0:T(8,128)S(1)}, f32[48,256]{1,0:T(8,128)S(1)}, u32[]{:S(2)}, u32[]{:S(2)}) %collective-permute-start.17) | collective-permute-done | bytes 49184 | tf_op jit(solution)/shard_map/ppermute | solution.py:14
  159.0 0.8 fusion.6
  159.9 1.6 fusion.2
  161.5 0.7 fusion.48
  162.2 2.5 collective-permute-start.18
  164.7 0.8 mul.180
  165.5 4.9 %collective-permute-start.19 = (f32[96,256]{1,0:T(8,128)}, f32[96,256]{1,0:T(8,128)S(1)}, u32[]{:S(2)}, u32[]{:S(2)}) collective-permute-start(f32[96,256]{1,0:T(8,128)} %get-tuple-element.14), channel_id=1, source_target_pairs={{4,0},{8,4},{12,8},{16,12},{20,16},{24,20},{28,24},{32,28},{36,32}... | collective-permute-start | bytes 294920 | tf_op jit(solution)/shard_map/ppermute | solution.py:14
  170.4 7.1 %collective-permute-start.20 = (f32[96,256]{1,0:T(8,128)S(1)}, f32[96,256]{1,0:T(8,128)S(1)}, u32[]{:S(2)}, u32[]{:S(2)}) collective-permute-start(f32[96,256]{1,0:T(8,128)S(1)} %get-tuple-element.13), channel_id=1, source_target_pairs={{0,64},{4,68},{8,72},{12,76},{16,80},{20,84},{24,88},{28,92},{32,9... | collective-permute-start | bytes 294920 | tf_op jit(solution)/shard_map/ppermute | solution.py:14
  177.5 1.3 collective-permute-start.21
  178.8 3.3 collective-permute-start.22
  182.2 1.4 collective-permute-start.23
  183.6 0.9 bitcast_dynamic-update-slice_fusion.5
  184.6 14.9 %collective-permute-done.21 = f32[96,256]{1,0:T(8,128)S(1)} collective-permute-done((f32[96,256]{1,0:T(8,128)S(1)}, f32[96,256]{1,0:T(8,128)S(1)}, u32[]{:S(2)}, u32[]{:S(2)}) %collective-permute-start.21) | collective-permute-done | bytes 98336 | tf_op jit(solution)/shard_map/ppermute | solution.py:14
  199.6 0.1 fusion.8
  199.8 0.5 convolution_bitcast_fusion
  200.3 9.3 %all_gather.7 = f32[192,256]{1,0:T(8,128)S(1)} all-gather(f32[48,256]{1,0:T(8,128)S(1)} %convolution_bitcast_fusion), channel_id=1, replica_groups=mesh['sub'=256,'grp'=4] {'grp'}, dimensions={0}, use_global_device_ids=true | all-gather | bytes 245760 | tf_op jit(solution)/shard_map/all_gather | solution.py:65
  209.6 0.3 fusion.16
  209.9 3.4 collective-permute-start.24
  213.4 1.6 fusion.4
  215.0 3.1 collective-permute-start.25
  218.1 6.1 %collective-permute-start.26 = (f32[48,256]{1,0:T(8,128)S(1)}, f32[48,256]{1,0:T(8,128)S(1)}, u32[]{:S(2)}, u32[]{:S(2)}) collective-permute-start(f32[48,256]{1,0:T(8,128)S(1)} %get-tuple-element.29), channel_id=1, source_target_pairs={{0,64},{4,68},{8,72},{12,76},{16,80},{20,84},{24,88},{28,92},{32,9... | collective-permute-start | bytes 147464 | tf_op jit(solution)/shard_map/ppermute | solution.py:14
  224.1 1.3 collective-permute-start.27
  225.5 14.7 %collective-permute-done.27 = f32[48,256]{1,0:T(8,128)S(1)} collective-permute-done((f32[48,256]{1,0:T(8,128)S(1)}, f32[48,256]{1,0:T(8,128)S(1)}, u32[]{:S(2)}, u32[]{:S(2)}) %collective-permute-start.27) | collective-permute-done | bytes 49184 | tf_op jit(solution)/shard_map/ppermute | solution.py:14
  240.3 0.7 multiply_subtract_fusion
  241.0 1.6 fusion
  242.6 0.3 multiply_reduce_fusion
  242.9 166.7 %psum.7 = f32[6,256]{1,0:T(8,128)S(1)} all-reduce(f32[6,256]{1,0:T(8,128)S(1)} %stack.173), channel_id=1, replica_groups=mesh['sub'=256,'grp'=4] {'sub','grp'}, use_global_device_ids=true, to_apply=%region_6.7 | all-reduce | flops 1536 | bytes 12288 | tf_op jit(solution)/shard_map/psum | solution.py:38
  409.6 1.3 fusion.7
  (84 shorter events, 0.5 us)
Async XLA Ops:
  0.6 159.2 %copy-start = (f32[1,1,576,576]{3,2,1,0:T(8,128)S(1)}, f32[1,1,576,576]{3,2,1,0:T(8,128)}, u32[]{:S(2)}) copy-start(f32[1,1,576,576]{3,2,1,0:T(8,128)} %param.6) | copy-start | bytes 3981316
  0.6 26.4 %copy-start.14 = (s32[1,1,6]{2,1,0:T(1,128)S(1)}, s32[1,1,6]{2,1,0:T(1,128)}, u32[]{:S(2)}) copy-start(s32[1,1,6]{2,1,0:T(1,128)} %param.11) | copy-start | bytes 76
  0.7 126.5 %collective-permute-start.12 = (f32[48,192]{1,0:T(8,128)}, f32[48,192]{1,0:T(8,128)S(1)}, u32[]{:S(2)}, u32[]{:S(2)}) collective-permute-start(f32[48,192]{1,0:T(8,128)} %bitcast.193), channel_id=1, source_target_pairs={{0,1},{1,2},{2,3},{4,5},{5,6},{6,7},{8,9},{9,10},{10,11},{12,13},{... | collective-permute-start | bytes 110600 | tf_op jit(solution)/shard_map/ppermute | solution.py:14
  4.7 122.4 %collective-permute-start.13 = (f32[48,192]{1,0:T(8,128)}, f32[48,192]{1,0:T(8,128)S(1)}, u32[]{:S(2)}, u32[]{:S(2)}) collective-permute-start(f32[48,192]{1,0:T(8,128)} %bitcast.194), channel_id=1, source_target_pairs={{1,0},{2,1},{3,2},{5,4},{6,5},{7,6},{9,8},{10,9},{11,10},{13,12},{... | collective-permute-start | bytes 110600 | tf_op jit(solution)/shard_map/ppermute | solution.py:14
  7.8 82.0 %collective-permute-start = (f32[96,256]{1,0:T(8,128)S(1)}, f32[96,256]{1,0:T(8,128)}, u32[]{:S(2)}, u32[]{:S(2)}) collective-permute-start(f32[96,256]{1,0:T(8,128)S(1)} %get-tuple-element.21), channel_id=1, source_target_pairs={{0,4},{4,8},{8,12},{12,16},{16,20},{20,24},{24,28},{28,32},{32,36}... | collective-permute-start | bytes 294920 | tf_op jit(solution)/shard_map/ppermute | solution.py:14
  12.2 79.8 %collective-permute-start.1 = (f32[96,256]{1,0:T(8,128)S(1)}, f32[96,256]{1,0:T(8,128)}, u32[]{:S(2)}, u32[]{:S(2)}) collective-permute-start(f32[96,256]{1,0:T(8,128)S(1)} %get-tuple-element.20), channel_id=1, source_target_pairs={{4,0},{8,4},{12,8},{16,12},{20,16},{24,20},{28,24},{32,28},{36,32}... | collective-permute-start | bytes 294920 | tf_op jit(solution)/shard_map/ppermute | solution.py:14
  24.8 90.2 %copy-start.1 = (f32[1,1,576,256]{3,2,1,0:T(8,128)S(1)}, f32[1,1,576,256]{3,2,1,0:T(8,128)}, u32[]{:S(2)}) copy-start(f32[1,1,576,256]{3,2,1,0:T(8,128)} %param.7) | copy-start | bytes 1769476
  24.9 90.2 %copy-start.4 = (f32[1,1,576,48]{2,3,1,0:T(8,128)S(1)}, f32[1,1,576,48]{2,3,1,0:T(8,128)}, u32[]{:S(2)}) copy-start(f32[1,1,576,48]{2,3,1,0:T(8,128)} %param.8) | copy-start | bytes 331780
  25.0 71.7 %copy-start.13 = (f32[96,256]{1,0:T(8,128)S(1)}, f32[96,256]{1,0:T(8,128)}, u32[]{:S(2)}) copy-start(f32[96,256]{1,0:T(8,128)} %get-tuple-element.16) | copy-start | bytes 294916
  25.0 3.3 collective-permute-start.6
  28.3 6.0 %collective-permute-start.7 = (f32[96,48]{1,0:T(8,128)S(1)}, f32[96,48]{1,0:T(8,128)S(1)}, u32[]{:S(2)}, u32[]{:S(2)}) collective-permute-start(f32[96,48]{1,0:T(8,128)S(1)} %get-tuple-element.26), channel_id=1, source_target_pairs={{4,0},{8,4},{12,8},{16,12},{20,16},{24,20},{28,24},{32,28},{36,32}... | collective-permute-start | bytes 55304 | tf_op jit(solution)/shard_map/ppermute | solution.py:14
  34.2 9.3 %collective-permute-start.8 = (f32[96,48]{1,0:T(8,128)S(1)}, f32[96,48]{1,0:T(8,128)S(1)}, u32[]{:S(2)}, u32[]{:S(2)}) collective-permute-start(f32[96,48]{1,0:T(8,128)S(1)} %get-tuple-element.25), channel_id=1, source_target_pairs={{0,64},{4,68},{8,72},{12,76},{16,80},{20,84},{24,88},{28,92},{32,9... | collective-permute-start | bytes 55304 | tf_op jit(solution)/shard_map/ppermute | solution.py:14
  43.6 28.0 %collective-permute-start.9 = (f32[96,48]{1,0:T(8,128)S(1)}, f32[96,48]{1,0:T(8,128)S(1)}, u32[]{:S(2)}, u32[]{:S(2)}) collective-permute-start(f32[96,48]{1,0:T(8,128)S(1)} %get-tuple-element.24), channel_id=1, source_target_pairs={{64,0},{68,4},{72,8},{76,12},{80,16},{84,20},{88,24},{92,28},{96,3... | collective-permute-start | bytes 55304 | tf_op jit(solution)/shard_map/ppermute | solution.py:14
  71.5 55.6 %copy-start.7 = (f32[1,1,48,192]{3,2,1,0:T(8,128)S(1)}, f32[1,1,48,192]{3,2,1,0:T(8,128)}, u32[]{:S(2)}) copy-start(f32[1,1,48,192]{3,2,1,0:T(8,128)} %param.9) | copy-start | bytes 110596
  71.5 5.6 %collective-permute-start.10 = (f32[96,48]{1,0:T(8,128)S(1)}, f32[96,48]{1,0:T(8,128)S(1)}, u32[]{:S(2)}, u32[]{:S(2)}) collective-permute-start(f32[96,48]{1,0:T(8,128)S(1)} %get-tuple-element.23), channel_id=1, source_target_pairs={{0,1},{1,2},{2,3},{4,5},{5,6},{6,7},{8,9},{9,10},{10,11},{12,13},{... | collective-permute-start | bytes 55304 | tf_op jit(solution)/shard_map/ppermute | solution.py:14
  77.1 19.6 %collective-permute-start.2 = (f32[96,256]{1,0:T(8,128)S(1)}, f32[96,256]{1,0:T(8,128)S(1)}, u32[]{:S(2)}, u32[]{:S(2)}) collective-permute-start(f32[96,256]{1,0:T(8,128)S(1)} %get-tuple-element.19), channel_id=1, source_target_pairs={{0,64},{4,68},{8,72},{12,76},{16,80},{20,84},{24,88},{28,92},{32,9... | collective-permute-start | bytes 294920 | tf_op jit(solution)/shard_map/ppermute | solution.py:14
  89.9 23.8 %collective-permute-start.3 = (f32[96,256]{1,0:T(8,128)S(1)}, f32[96,256]{1,0:T(8,128)S(1)}, u32[]{:S(2)}, u32[]{:S(2)}) collective-permute-start(f32[96,256]{1,0:T(8,128)S(1)} %get-tuple-element.18), channel_id=1, source_target_pairs={{64,0},{68,4},{72,8},{76,12},{80,16},{84,20},{88,24},{92,28},{96,3... | collective-permute-start | bytes 294920 | tf_op jit(solution)/shard_map/ppermute | solution.py:14
  92.1 22.9 %collective-permute-start.4 = (f32[96,256]{1,0:T(8,128)S(1)}, f32[96,256]{1,0:T(8,128)S(1)}, u32[]{:S(2)}, u32[]{:S(2)}) collective-permute-start(f32[96,256]{1,0:T(8,128)S(1)} %get-tuple-element.17), channel_id=1, source_target_pairs={{0,1},{1,2},{2,3},{4,5},{5,6},{6,7},{8,9},{9,10},{10,11},{12,13},{... | collective-permute-start | bytes 294920 | tf_op jit(solution)/shard_map/ppermute | solution.py:14
  96.7 18.4 %collective-permute-start.5 = (f32[96,256]{1,0:T(8,128)S(1)}, f32[96,256]{1,0:T(8,128)S(1)}, u32[]{:S(2)}, u32[]{:S(2)}) collective-permute-start(f32[96,256]{1,0:T(8,128)S(1)} %copy-done.13), channel_id=1, source_target_pairs={{1,0},{2,1},{3,2},{5,4},{6,5},{7,6},{9,8},{10,9},{11,10},{13,12},{... | collective-permute-start | bytes 294920 | tf_op jit(solution)/shard_map/ppermute | solution.py:14
  113.7 17.0 %collective-permute-start.11 = (f32[96,48]{1,0:T(8,128)S(1)}, f32[96,48]{1,0:T(8,128)S(1)}, u32[]{:S(2)}, u32[]{:S(2)}) collective-permute-start(f32[96,48]{1,0:T(8,128)S(1)} %get-tuple-element.22), channel_id=1, source_target_pairs={{1,0},{2,1},{3,2},{5,4},{6,5},{7,6},{9,8},{10,9},{11,10},{13,12},{... | collective-permute-start | bytes 55304 | tf_op jit(solution)/shard_map/ppermute | solution.py:14
  127.1 31.8 %copy-start.9 = (f32[48,192]{1,0:T(8,128)}, f32[48,192]{1,0:T(8,128)S(1)}, u32[]{:S(2)}) copy-start(f32[48,192]{1,0:T(8,128)S(1)} %collective-permute-done.12) | copy-start | bytes 110596
  127.2 31.8 %copy-start.11 = (f32[48,192]{1,0:T(8,128)}, f32[48,192]{1,0:T(8,128)S(1)}, u32[]{:S(2)}) copy-start(f32[48,192]{1,0:T(8,128)S(1)} %collective-permute-done.13) | copy-start | bytes 110596
  127.5 18.5 %collective-permute-start.14 = (f32[48,256]{1,0:T(8,128)S(1)}, f32[48,256]{1,0:T(8,128)S(1)}, u32[]{:S(2)}, u32[]{:S(2)}) collective-permute-start(f32[48,256]{1,0:T(8,128)S(1)} %get-tuple-element.31), channel_id=1, source_target_pairs={{0,4},{4,8},{8,12},{12,16},{16,20},{20,24},{24,28},{28,32},{32,36}... | collective-permute-start | bytes 147464 | tf_op jit(solution)/shard_map/ppermute | solution.py:14
  130.8 29.1 %copy-start.2 = (f32[6,96,48]{2,1,0:T(8,128)}, f32[6,96,48]{2,1,0:T(8,128)S(1)}, u32[]{:S(2)}) copy-start(f32[6,96,48]{2,1,0:T(8,128)S(1)} %neg.6) | copy-start | bytes 331780
  130.8 15.2 %collective-permute-start.15 = (f32[48,256]{1,0:T(8,128)S(1)}, f32[48,256]{1,0:T(8,128)S(1)}, u32[]{:S(2)}, u32[]{:S(2)}) collective-permute-start(f32[48,256]{1,0:T(8,128)S(1)} %get-tuple-element.31), channel_id=1, source_target_pairs={{4,0},{8,4},{12,8},{16,12},{20,16},{24,20},{28,24},{32,28},{36,32}... | collective-permute-start | bytes 147464 | tf_op jit(solution)/shard_map/ppermute | solution.py:14
  133.9 14.5 %collective-permute-start.16 = (f32[48,256]{1,0:T(8,128)S(1)}, f32[48,256]{1,0:T(8,128)S(1)}, u32[]{:S(2)}, u32[]{:S(2)}) collective-permute-start(f32[48,256]{1,0:T(8,128)S(1)} %get-tuple-element.31), channel_id=1, source_target_pairs={{0,64},{4,68},{8,72},{12,76},{16,80},{20,84},{24,88},{28,92},{32,9... | collective-permute-start | bytes 147464 | tf_op jit(solution)/shard_map/ppermute | solution.py:14
  144.6 14.3 %collective-permute-start.17 = (f32[48,256]{1,0:T(8,128)S(1)}, f32[48,256]{1,0:T(8,128)S(1)}, u32[]{:S(2)}, u32[]{:S(2)}) collective-permute-start(f32[48,256]{1,0:T(8,128)S(1)} %get-tuple-element.31), channel_id=1, source_target_pairs={{64,0},{68,4},{72,8},{76,12},{80,16},{84,20},{88,24},{92,28},{96,3... | collective-permute-start | bytes 147464 | tf_op jit(solution)/shard_map/ppermute | solution.py:14
  159.8 4.8 %copy-start.5 = (f32[1,1,576,48]{2,3,1,0:T(8,128)S(1)}, f32[1,1,576,48]{2,3,1,0:T(8,128)}, u32[]{:S(2)}) copy-start(f32[1,1,576,48]{2,3,1,0:T(8,128)} %param.8) | copy-start | bytes 331780
  162.2 20.0 %collective-permute-start.18 = (f32[96,256]{1,0:T(8,128)}, f32[96,256]{1,0:T(8,128)}, u32[]{:S(2)}, u32[]{:S(2)}) collective-permute-start(f32[96,256]{1,0:T(8,128)} %get-tuple-element.15), channel_id=1, source_target_pairs={{0,4},{4,8},{8,12},{12,16},{16,20},{20,24},{24,28},{28,32},{32,36}... | collective-permute-start | bytes 294920 | tf_op jit(solution)/shard_map/ppermute | solution.py:14
  165.5 19.1 %collective-permute-start.19 = (f32[96,256]{1,0:T(8,128)}, f32[96,256]{1,0:T(8,128)S(1)}, u32[]{:S(2)}, u32[]{:S(2)}) collective-permute-start(f32[96,256]{1,0:T(8,128)} %get-tuple-element.14), channel_id=1, source_target_pairs={{4,0},{8,4},{12,8},{16,12},{20,16},{24,20},{28,24},{32,28},{36,32}... | collective-permute-start | bytes 294920 | tf_op jit(solution)/shard_map/ppermute | solution.py:14
  170.4 14.1 %collective-permute-start.20 = (f32[96,256]{1,0:T(8,128)S(1)}, f32[96,256]{1,0:T(8,128)S(1)}, u32[]{:S(2)}, u32[]{:S(2)}) collective-permute-start(f32[96,256]{1,0:T(8,128)S(1)} %get-tuple-element.13), channel_id=1, source_target_pairs={{0,64},{4,68},{8,72},{12,76},{16,80},{20,84},{24,88},{28,92},{32,9... | collective-permute-start | bytes 294920 | tf_op jit(solution)/shard_map/ppermute | solution.py:14
  177.5 22.0 %collective-permute-start.21 = (f32[96,256]{1,0:T(8,128)S(1)}, f32[96,256]{1,0:T(8,128)S(1)}, u32[]{:S(2)}, u32[]{:S(2)}) collective-permute-start(f32[96,256]{1,0:T(8,128)S(1)} %get-tuple-element.12), channel_id=1, source_target_pairs={{64,0},{68,4},{72,8},{76,12},{80,16},{84,20},{88,24},{92,28},{96,3... | collective-permute-start | bytes 294920 | tf_op jit(solution)/shard_map/ppermute | solution.py:14
  178.8 20.7 %collective-permute-start.22 = (f32[96,256]{1,0:T(8,128)S(1)}, f32[96,256]{1,0:T(8,128)S(1)}, u32[]{:S(2)}, u32[]{:S(2)}) collective-permute-start(f32[96,256]{1,0:T(8,128)S(1)} %get-tuple-element.11), channel_id=1, source_target_pairs={{0,1},{1,2},{2,3},{4,5},{5,6},{6,7},{8,9},{9,10},{10,11},{12,13},{... | collective-permute-start | bytes 294920 | tf_op jit(solution)/shard_map/ppermute | solution.py:14
  182.2 17.6 %copy-start.6 = (f32[6,96,48]{1,0,2:T(8,128)S(1)}, f32[6,96,48]{1,0,2:T(8,128)}, u32[]{:S(2)}) copy-start(f32[6,96,48]{1,0,2:T(8,128)} %mul.180) | copy-start | bytes 331780
  182.2 17.4 %collective-permute-start.23 = (f32[96,256]{1,0:T(8,128)S(1)}, f32[96,256]{1,0:T(8,128)S(1)}, u32[]{:S(2)}, u32[]{:S(2)}) collective-permute-start(f32[96,256]{1,0:T(8,128)S(1)} %get-tuple-element.10), channel_id=1, source_target_pairs={{1,0},{2,1},{3,2},{5,4},{6,5},{7,6},{9,8},{10,9},{11,10},{13,12},{... | collective-permute-start | bytes 294920 | tf_op jit(solution)/shard_map/ppermute | solution.py:14
  199.6 10.0 %copy-start.8 = (f32[1,1,48,192]{3,2,1,0:T(8,128)S(1)}, f32[1,1,48,192]{3,2,1,0:T(8,128)}, u32[]{:S(2)}) copy-start(f32[1,1,48,192]{3,2,1,0:T(8,128)} %param.9) | copy-start | bytes 110596
  199.6 10.0 %copy-start.10 = (f32[48,192]{1,0:T(8,128)S(1)}, f32[48,192]{1,0:T(8,128)}, u32[]{:S(2)}) copy-start(f32[48,192]{1,0:T(8,128)} %copy-done.9) | copy-start | bytes 110596
  199.6 10.0 %copy-start.12 = (f32[48,192]{1,0:T(8,128)S(1)}, f32[48,192]{1,0:T(8,128)}, u32[]{:S(2)}) copy-start(f32[48,192]{1,0:T(8,128)} %copy-done.11) | copy-start | bytes 110596
  209.9 15.5 %collective-permute-start.24 = (f32[48,256]{1,0:T(8,128)S(1)}, f32[48,256]{1,0:T(8,128)S(1)}, u32[]{:S(2)}, u32[]{:S(2)}) collective-permute-start(f32[48,256]{1,0:T(8,128)S(1)} %get-tuple-element.29), channel_id=1, source_target_pairs={{0,4},{4,8},{8,12},{12,16},{16,20},{20,24},{24,28},{28,32},{32,36}... | collective-permute-start | bytes 147464 | tf_op jit(solution)/shard_map/ppermute | solution.py:14
  213.4 26.9 %copy-start.3 = (f32[6,96,48]{2,1,0:T(8,128)S(1)}, f32[6,96,48]{2,1,0:T(8,128)}, u32[]{:S(2)}) copy-start(f32[6,96,48]{2,1,0:T(8,128)} %copy-done.2) | copy-start | bytes 331780
  215.0 10.5 %collective-permute-start.25 = (f32[48,256]{1,0:T(8,128)S(1)}, f32[48,256]{1,0:T(8,128)S(1)}, u32[]{:S(2)}, u32[]{:S(2)}) collective-permute-start(f32[48,256]{1,0:T(8,128)S(1)} %get-tuple-element.29), channel_id=1, source_target_pairs={{4,0},{8,4},{12,8},{16,12},{20,16},{24,20},{28,24},{32,28},{36,32}... | collective-permute-start | bytes 147464 | tf_op jit(solution)/shard_map/ppermute | solution.py:14
  218.1 7.4 %collective-permute-start.26 = (f32[48,256]{1,0:T(8,128)S(1)}, f32[48,256]{1,0:T(8,128)S(1)}, u32[]{:S(2)}, u32[]{:S(2)}) collective-permute-start(f32[48,256]{1,0:T(8,128)S(1)} %get-tuple-element.29), channel_id=1, source_target_pairs={{0,64},{4,68},{8,72},{12,76},{16,80},{20,84},{24,88},{28,92},{32,9... | collective-permute-start | bytes 147464 | tf_op jit(solution)/shard_map/ppermute | solution.py:14
  224.1 16.1 %collective-permute-start.27 = (f32[48,256]{1,0:T(8,128)S(1)}, f32[48,256]{1,0:T(8,128)S(1)}, u32[]{:S(2)}, u32[]{:S(2)}) collective-permute-start(f32[48,256]{1,0:T(8,128)S(1)} %get-tuple-element.29), channel_id=1, source_target_pairs={{64,0},{68,4},{72,8},{76,12},{80,16},{84,20},{88,24},{92,28},{96,3... | collective-permute-start | bytes 147464 | tf_op jit(solution)/shard_map/ppermute | solution.py:14

commit v2 on v1

v2 whole, which is shorter than its diff:
```python
import jax
import jax.numpy as jnp
from jax import lax
from jax.sharding import Mesh, PartitionSpec as P


SUBROW = 16
PLANE = ("y", "core", "grp")
SUB = ("y", "z", "core")
SOURCES = ((SUB, -1), (SUB, 1), (SUB, -SUBROW), (SUB, SUBROW), ("grp", -1), ("grp", 1))
ORDER = (2, 3, 0, 1, 4, 5)


def fetch(piece, slot):
    axis, offset = SOURCES[slot]
    count = lax.axis_size(axis)
    pairs = [(i, i - offset) for i in range(count) if 0 <= i - offset < count]
    return lax.ppermute(piece, axis, pairs)


def exchange(pieces):
    gotten = [None] * len(pieces)
    for slot in ORDER:
        if slot < len(pieces):
            gotten[slot] = fetch(pieces[slot], slot)
    return gotten


def matmul(left, right):
    return jnp.dot(left, right, precision=lax.Precision.HIGHEST, preferred_element_type=jnp.float32)


def clamp(values, upper, lower):
    return jnp.where(upper, jnp.maximum(values, 0.0), jnp.where(lower, jnp.minimum(values, 0.0), values))


def swap(blocks, axes):
    return lax.all_to_all(blocks, axes, 0, 0, tiled=True)


def total(terms):
    plane = lax.axis_size(PLANE)
    chunks = terms.reshape(plane, -1)
    chunk = jnp.sum(swap(chunks, PLANE), axis=0)
    chunk = jnp.sum(swap(jnp.broadcast_to(chunk, (lax.axis_size("z"),) + chunk.shape), "z"), axis=0)
    return swap(jnp.broadcast_to(chunk, chunks.shape), PLANE).reshape(terms.shape)


def gather(block):
    count = lax.axis_size("grp")
    return swap(jnp.broadcast_to(block, (count,) + block.shape), "grp").reshape(-1, block.shape[-1])


def body(dual_ops, gap_parts, modes, coarse_rows, face_live, contact):
    operator = dual_ops[0, 0]
    dual_rows = operator.shape[0]
    face_rows = dual_rows // 6
    cases = gap_parts.shape[3]
    kinds = modes.shape[3]
    half = kinds // 2
    lanes = cases // 2
    live_flags = face_live[0, 0].astype(jnp.float32)
    live_view = live_flags[:, None, None]
    parity = jnp.arange(6) % 2
    upper = (contact[0, 0] * parity)[:, None, None] > 0
    lower = (contact[0, 0] * (1 - parity))[:, None, None] > 0
    own_rows = coarse_rows[0, 0]
    parts = gap_parts[0, 0].reshape(6, face_rows, cases)
    shapes = modes[0, 0].T.reshape(kinds, 6, face_rows)

    messages = []
    for slot in range(6):
        wide = jnp.pad(shapes[:, slot ^ 1], ((0, 0), (0, lanes - face_rows)))
        message = [parts[slot ^ 1], jnp.concatenate([wide[:half], wide[half:]], axis=1)]
        if slot >= 4:
            message.append(jnp.pad(own_rows, ((0, 0), (0, cases - own_rows.shape[1]))))
        messages.append(jnp.concatenate(message))
    gotten = exchange(messages)
    parts_across = jnp.stack([message[:face_rows] for message in gotten])
    pairs = []
    for slot in range(6):
        packed = gotten[slot][face_rows:face_rows + half]
        other = jnp.concatenate([packed[:, :face_rows], packed[:, lanes:lanes + face_rows]])
        pairs.append(live_flags[slot] * jnp.concatenate([shapes[:, slot], -other]))
    pairs = jnp.stack(pairs)
    masked = jnp.repeat(live_flags, face_rows)[None, :] * shapes.reshape(kinds, dual_rows)
    near_rows = [gotten[slot][face_rows + half:, :own_rows.shape[1]] for slot in (4, 5)]
    all_rows = jnp.concatenate([own_rows] + near_rows)

    def projected(values):
        coef = matmul(masked, values.reshape(dual_rows, cases))
        coarse = matmul(all_rows, gather(coef))
        own = coarse[:kinds]
        near = exchange([own] * 4) + [coarse[kinds:2 * kinds], coarse[2 * kinds:]]
        stacked = jnp.stack([jnp.concatenate([own, other]) for other in near])
        correction = jnp.einsum(
            "kmi,kml->kil", pairs, stacked, precision=lax.Precision.HIGHEST, preferred_element_type=jnp.float32
        )
        return values - correction

    def apply_local(values):
        return matmul(operator, values.reshape(dual_rows, cases)).reshape(6, face_rows, cases)

    first = projected(live_view * (parts_across - parts))
    push = clamp(-first, upper, lower)
    pushed = apply_local(push)
    first_image = apply_local(first)
    pushed_across = jnp.stack(exchange([pushed[slot ^ 1] for slot in range(6)]))
    change = projected(live_view * (pushed - pushed_across))
    change_image = apply_local(change)

    def inner(left, right):
        return jnp.sum(left * right, axis=(0, 1))

    sums = total(jnp.stack([
        inner(first, first), inner(first, first_image), inner(first, change),
        inner(change, change), inner(change, first_image), inner(change, change_image),
    ]))
    step = sums[0] / (2.0 * sums[1])
    norm = sums[0] + step * (2.0 * sums[2] + step * sums[3])
    curvature = 2.0 * (sums[1] + step * (2.0 * sums[4] + step * sums[5]))
    direction = first + step * change
    multipliers = clamp(step * push - (norm / curvature) * direction, upper, lower)
    shape = (1, 1, dual_rows, cases)
    return (multipliers.reshape(shape), direction.reshape(shape))


def solution(mesh):
    fine = Mesh(mesh.devices.reshape(4, 32, 2, 4), ("y", "z", "core", "grp"))
    wide = P(SUB, "grp", None, None)
    flags = P(SUB, "grp", None)
    return jax.shard_map(
        body, mesh=fine, in_specs=(wide, wide, wide, wide, flags, flags), out_specs=(wide, wide), check_vma=False
    )
```

time: 412 us -> 312 us (0.76)
  blocking collectives: 187 us -> 68.5 us
  local copies, waits for them, and re-layouts: 7.5 us -> 40.3 us
  starting transfers between devices: 112 us -> 91.1 us
  waiting for transfers between devices: 92.2 us -> 72.7 us
  matrix products: 7.98 us -> 21.5 us
  other arithmetic: 2.62 us -> 14.6 us
    psum x1 -> x0, blocking collectives: 167 us -> none  [total(): return lax.psum(terms, ('sub', 'grp'))]
    all_to_all x0 -> x3, blocking collectives: none -> 68.5 us  [swap(): return lax.all_to_all(blocks, axes, 0, 0, tiled=True)]
    ppermute x28 -> x20, starting transfers between devices: 112 us -> 82.9 us  [fetch(): return lax.ppermute(piece, axis, pairs)]
    ppermute x28 -> x20, waiting for transfers between devices: 92.2 us -> 67.3 us  [fetch(): return lax.ppermute(piece, axis, pairs)]
    all_gather x2 -> x0, blocking collectives: 20.8 us -> none  [projected(): coarse = matmul(all_rows, lax.all_gather(coef, 'grp', axis=0, tiled=True))]
    dot_general x7, matrix products: 6.4 us -> 15.1 us  [matmul(): jnp.dot(left, right, precision=lax.Precision.HIGHEST, preferred_element_t...]
    all_to_all x0 -> x2, starting transfers between devices: none -> 8.19 us  [swap(): return lax.all_to_all(blocks, axes, 0, 0, tiled=True)]
    another operation x3 -> x7, local copies, waits for them, and re-layouts: 0.03 us -> 7.52 us  [the longest x3 3.23 us: body(): parts_across = jnp.stack([message[:face_rows] for message in gotten])]
  transfers between devices with their start and end apart: 28 -> 22, of which waited for: 10 -> 7; matrix products, arithmetic and copies ran while one was open for 2% -> 10% of each run, Pallas kernels for 0% -> 0%
where the time goes in v2:
time: 312 us; the launch traced here: 310 us
  starting transfers between devices  91.1 us (29%)
  waiting for transfers between devices  72.7 us (23%)
  blocking collectives  68.5 us (22%)
  local copies, waits for them, and re-layouts  40.3 us (13%)
  matrix products  21.5 us (7%)
  other arithmetic  14.6 us (5%)
    ppermute x20, starting transfers between devices, fetch(): return lax.ppermute(piece, axis, pairs)  82.9 us
    all_to_all x3, blocking collectives, swap(): return lax.all_to_all(blocks, axes, 0, 0, tiled=True)  68.5 us
    ppermute x20, waiting for transfers between devices, fetch(): return lax.ppermute(piece, axis, pairs)  67.3 us
    dot_general x7, matrix products, matmul(): jnp.dot(left, right, precision=lax.Precision.HIGHEST, preferred_element_t...  15.1 us
    unnamed x76, local copies, waits for them, and re-layouts  9.83 us
    all_to_all x2, starting transfers between devices, swap(): return lax.all_to_all(blocks, axes, 0, 0, tiled=True)  8.19 us
    dot_general x2, matrix products, projected(): jnp.einsum('kmi,kml->kil', pairs, stacked, precision=lax.Precision.HIGHES...  6.46 us
  transfers between devices with their start and end apart: 22, of which 7 were waited for; matrix products, arithmetic and copies ran while one was open for 10% of the time, Pallas kernels for 0%

profile of v2, /device:TPU:1, one launch (start us, length us, event | category | flops | bytes accessed | tf_op | source)
XLA Modules:
  0.0 310.4 jit_solution(48983348730244626)
XLA Ops:
  0.7 1.2 copy.121
  3.9 16.0 %collective-permute-start.1 = (f32[120,256]{0,1:T(8,128)}, f32[120,256]{0,1:T(8,128)S(1)}, u32[]{:S(2)}, u32[]{:S(2)}) collective-permute-start(f32[120,256]{0,1:T(8,128)} %maximum_maximum_fusion.1), channel_id=1, source_target_pairs={{4,0},{8,4},{12,8},{16,12},{20,16},{24,20},{28,24},{32,28},{36,32}... | collective-permute-start | bytes 368648 | tf_op jit(solution)/shard_map/ppermute | solution.py:18
  20.7 2.0 collective-permute-start
  23.6 4.3 %collective-permute-start.2 = (f32[120,256]{0,1:T(8,128)}, f32[120,256]{0,1:T(8,128)S(1)}, u32[]{:S(2)}, u32[]{:S(2)}) collective-permute-start(f32[120,256]{0,1:T(8,128)} %maximum_maximum_fusion.2), channel_id=1, source_target_pairs={{0,64},{4,68},{8,72},{12,76},{16,80},{20,84},{24,88},{28,92},{32,9... | collective-permute-start | bytes 368648 | tf_op jit(solution)/shard_map/ppermute | solution.py:18
  28.7 1.3 collective-permute-start.3
  30.9 1.0 pad_slice_fusion.1
  31.9 1.1 fusion.20
  32.9 3.9 %collective-permute-start.4 = (f32[168,256]{0,1:T(8,128)}, f32[168,256]{0,1:T(8,128)}, u32[]{:S(2)}, u32[]{:S(2)}) collective-permute-start(f32[168,256]{0,1:T(8,128)} %get-tuple-element.53), channel_id=1, source_target_pairs={{0,1},{1,2},{2,3},{4,5},{5,6},{6,7},{8,9},{9,10},{10,11},{12,13},{... | collective-permute-start | bytes 516104 | tf_op jit(solution)/shard_map/ppermute | solution.py:18
  37.7 1.2 copy.128
  39.5 1.3 collective-permute-start.5
  41.4 26.0 %collective-permute-done.3 = f32[120,256]{0,1:T(8,128)} collective-permute-done((f32[120,256]{0,1:T(8,128)}, f32[120,256]{0,1:T(8,128)}, u32[]{:S(2)}, u32[]{:S(2)}) %collective-permute-start.3) | collective-permute-done | bytes 122912 | tf_op jit(solution)/shard_map/ppermute | solution.py:18
  71.4 0.9 fusion.26
  72.3 0.9 fusion.25
  73.2 0.9 fusion.24
  74.1 0.9 fusion.23
  75.1 0.9 fusion.22
  76.7 1.1 copy.129
  77.8 2.1 copy.131
  79.9 1.8 fusion.12
  82.4 4.0 %all-to-all-start = ((f32[4,48,256]{2,1,0:T(8,128)}), f32[4,48,256]{2,1,0:T(8,128)S(1)}, u32[]{:S(2)}, u32[]{:S(2)}) async-start(f32[4,48,256]{2,1,0:T(8,128)} %broadcast_in_dim.42), calls=%async_computation | async-start | bytes 393216 | tf_op jit(solution)/shard_map/all_to_all | solution.py:38
  87.5 0.9 fusion.68
  88.5 1.0 slice.342
  89.5 1.0 slice.343
  92.3 2.6 collective-permute-start.6
  95.6 2.4 collective-permute-start.7
  98.1 12.9 %collective-permute-start.8 = (f32[48,256]{1,0:T(8,128)S(1)}, f32[48,256]{1,0:T(8,128)S(1)}, u32[]{:S(2)}, u32[]{:S(2)}) collective-permute-start(f32[48,256]{1,0:T(8,128)S(1)} %get-tuple-element.43), channel_id=1, source_target_pairs={{0,64},{4,68},{8,72},{12,76},{16,80},{20,84},{24,88},{28,92},{32,9... | collective-permute-start | bytes 147464 | tf_op jit(solution)/shard_map/ppermute | solution.py:18
  111.0 1.3 collective-permute-start.9
  112.4 12.2 %collective-permute-done.9 = f32[48,256]{1,0:T(8,128)S(1)} collective-permute-done((f32[48,256]{1,0:T(8,128)S(1)}, f32[48,256]{1,0:T(8,128)S(1)}, u32[]{:S(2)}, u32[]{:S(2)}) %collective-permute-start.9) | collective-permute-done | bytes 49184 | tf_op jit(solution)/shard_map/ppermute | solution.py:18
  124.6 3.7 %fusion.9 = (f32[6,96,256]{1,2,0:T(8,128)}, f32[6,96,256]{1,2,0:T(8,128)S(1)}) fusion(pred[6]{0:T(512)(128)(4,1)S(1)} %get-tuple-element.77, pred[6]{0:T(512)(128)(4,1)S(1)} %get-tuple-element.76, f32[6,96,256]{1,2,0:T(8,128)S(1)} %fusion.21, f32[6,96,256]{1,2,0:T(8,128)} %copy.128, f32[6]{0:T(128)S(1)} %get-tuple-element.74, ...), kind=kOutput, calls=%fused_computation.9 | convolution fusion | flops 171048960 | bytes 3170340 | tf_op jit(solution)/shard_map/kmi,kml->kil/dot_general | solution.py:96
  128.4 1.4 copy.135
  129.8 3.3 %fusion.6 = f32[576,256]{0,1:T(8,128)S(1)} fusion(f32[576,256]{1,0:T(8,128)S(1)} %bitcast.221, f32[1,1,576,576]{3,2,1,0:T(8,128)S(1)} %copy-done), kind=kOutput, calls=%fused_computation.6 | convolution fusion | flops 1019215872 | bytes 2506752 | tf_op jit(solution)/shard_map/dot_general | solution.py:30
  133.2 3.4 %collective-permute-start.10 = (f32[96,256]{0,1:T(8,128)S(1)}, f32[96,256]{0,1:T(8,128)S(1)}, u32[]{:S(2)}, u32[]{:S(2)}) collective-permute-start(f32[96,256]{0,1:T(8,128)S(1)} %get-tuple-element.17), channel_id=1, source_target_pairs={{0,4},{4,8},{8,12},{12,16},{16,20},{20,24},{24,28},{28,32},{32,36}... | collective-permute-start | bytes 294920 | tf_op jit(solution)/shard_map/ppermute | solution.py:18
  136.7 4.2 %collective-permute-start.11 = (f32[96,256]{0,1:T(8,128)S(1)}, f32[96,256]{0,1:T(8,128)S(1)}, u32[]{:S(2)}, u32[]{:S(2)}) collective-permute-start(f32[96,256]{0,1:T(8,128)S(1)} %get-tuple-element.16), channel_id=1, source_target_pairs={{4,0},{8,4},{12,8},{16,12},{20,16},{24,20},{28,24},{32,28},{36,32}... | collective-permute-start | bytes 294920 | tf_op jit(solution)/shard_map/ppermute | solution.py:18
  140.9 6.6 %collective-permute-start.12 = (f32[96,256]{0,1:T(8,128)S(1)}, f32[96,256]{0,1:T(8,128)S(1)}, u32[]{:S(2)}, u32[]{:S(2)}) collective-permute-start(f32[96,256]{0,1:T(8,128)S(1)} %get-tuple-element.15), channel_id=1, source_target_pairs={{0,64},{4,68},{8,72},{12,76},{16,80},{20,84},{24,88},{28,92},{32,9... | collective-permute-start | bytes 294920 | tf_op jit(solution)/shard_map/ppermute | solution.py:18
  147.5 1.3 collective-permute-start.13
  148.8 2.2 collective-permute-start.14
  151.0 1.3 collective-permute-start.15
  153.6 8.8 %collective-permute-done.12 = f32[96,256]{0,1:T(8,128)S(1)} collective-permute-done((f32[96,256]{0,1:T(8,128)S(1)}, f32[96,256]{0,1:T(8,128)S(1)}, u32[]{:S(2)}, u32[]{:S(2)}) %collective-permute-start.12) | collective-permute-done | bytes 98336 | tf_op jit(solution)/shard_map/ppermute | solution.py:18
  163.0 8.0 %collective-permute-done.13 = f32[96,256]{0,1:T(8,128)S(1)} collective-permute-done((f32[96,256]{0,1:T(8,128)S(1)}, f32[96,256]{0,1:T(8,128)S(1)}, u32[]{:S(2)}, u32[]{:S(2)}) %collective-permute-start.13) | collective-permute-done | bytes 98336 | tf_op jit(solution)/shard_map/ppermute | solution.py:18
  173.0 1.4 copy.139
  174.4 1.1 copy.140
  175.5 1.8 fusion.14
  178.1 4.2 %all-to-all-start.1 = ((f32[4,48,256]{2,1,0:T(8,128)}), f32[4,48,256]{2,1,0:T(8,128)}, u32[]{:S(2)}, u32[]{:S(2)}) async-start(f32[4,48,256]{2,1,0:T(8,128)} %broadcast_in_dim.44), calls=%async_computation.1 | async-start | bytes 393216 | tf_op jit(solution)/shard_map/all_to_all | solution.py:38
  182.5 5.0 %all-to-all-done.1 = f32[4,48,256]{2,1,0:T(8,128)} async-done(((f32[4,48,256]{2,1,0:T(8,128)}), f32[4,48,256]{2,1,0:T(8,128)}, u32[]{:S(2)}, u32[]{:S(2)}) %all-to-all-start.1) | async-done | bytes 196640 | tf_op jit(solution)/shard_map/all_to_all | solution.py:38
  187.5 1.7 fusion.51
  189.9 1.9 collective-permute-start.16
  191.8 2.4 fusion.4
  194.4 1.2 copy.138
  195.6 1.2 copy.134
  196.8 3.6 %collective-permute-start.17 = (f32[48,256]{1,0:T(8,128)S(1)}, f32[48,256]{1,0:T(8,128)S(1)}, u32[]{:S(2)}, u32[]{:S(2)}) collective-permute-start(f32[48,256]{1,0:T(8,128)S(1)} %get-tuple-element.41), channel_id=1, source_target_pairs={{4,0},{8,4},{12,8},{16,12},{20,16},{24,20},{28,24},{32,28},{36,32}... | collective-permute-start | bytes 147464 | tf_op jit(solution)/shard_map/ppermute | solution.py:18
  200.3 9.1 %collective-permute-start.18 = (f32[48,256]{1,0:T(8,128)S(1)}, f32[48,256]{1,0:T(8,128)S(1)}, u32[]{:S(2)}, u32[]{:S(2)}) collective-permute-start(f32[48,256]{1,0:T(8,128)S(1)} %get-tuple-element.41), channel_id=1, source_target_pairs={{0,64},{4,68},{8,72},{12,76},{16,80},{20,84},{24,88},{28,92},{32,9... | collective-permute-start | bytes 147464 | tf_op jit(solution)/shard_map/ppermute | solution.py:18
  209.4 1.3 collective-permute-start.19
  211.6 12.3 %collective-permute-done.19 = f32[48,256]{1,0:T(8,128)S(1)} collective-permute-done((f32[48,256]{1,0:T(8,128)S(1)}, f32[48,256]{1,0:T(8,128)S(1)}, u32[]{:S(2)}, u32[]{:S(2)}) %collective-permute-start.19) | collective-permute-done | bytes 49184 | tf_op jit(solution)/shard_map/ppermute | solution.py:18
  223.9 2.7 multiply_subtract_fusion
  226.7 1.1 copy.143
  227.7 3.4 %fusion = f32[256,576]{0,1:T(8,128)} fusion(f32[576,256]{1,0:T(8,128)} %bitcast.223, f32[1,1,576,576]{3,2,1,0:T(8,128)S(1)} %copy-done), kind=kOutput, calls=%fused_computation | convolution fusion | flops 1019215872 | bytes 2506752 | tf_op jit(solution)/shard_map/dot_general | solution.py:30
  231.2 2.2 copy.144
  233.4 1.9 multiply_reduce_fusion
  235.5 21.2 %all_to_all.31 = f32[32,1,48]{2,1,0:T(1,128)S(1)} all-to-all(f32[32,1,48]{2,1,0:T(1,128)S(1)} %all_to_all.22), channel_id=1, replica_groups=mesh['y'=4,'z'=32,'core'=2,'grp'=4] {'y','core','grp'}, dimensions={0} | all-to-all | bytes 12288 | tf_op jit(solution)/shard_map/all_to_all | solution.py:38
  256.7 35.3 %all_to_all.32 = f32[32,1,48]{2,1,0:T(1,128)S(1)} all-to-all(f32[32,1,48]{2,1,0:T(1,128)S(1)} %broadcast_in_dim.45), channel_id=1, replica_groups=mesh['y'=4,'z'=32,'core'=2,'grp'=4] {'z'}, dimensions={0} | all-to-all | bytes 12288 | tf_op jit(solution)/shard_map/all_to_all | solution.py:38
  292.1 12.0 %all_to_all.33 = f32[32,1,48]{2,1,0:T(1,128)S(1)} all-to-all(f32[32,1,48]{2,1,0:T(1,128)S(1)} %broadcast_in_dim.46), channel_id=1, replica_groups=mesh['y'=4,'z'=32,'core'=2,'grp'=4] {'y','core','grp'}, dimensions={0} | all-to-all | bytes 12288 | tf_op jit(solution)/shard_map/all_to_all | solution.py:38
  305.4 1.6 fusion.10
  307.0 2.3 copy.146
  309.3 1.1 copy.147
  (148 shorter events, 24.5 us)
Async XLA Ops:
  0.6 129.1 %copy-start = (f32[1,1,576,576]{3,2,1,0:T(8,128)S(1)}, f32[1,1,576,576]{3,2,1,0:T(8,128)}, u32[]{:S(2)}) copy-start(f32[1,1,576,576]{3,2,1,0:T(8,128)} %param.6) | copy-start | bytes 3981316
  0.6 2.0 copy-start.3
  3.9 37.0 %collective-permute-start.1 = (f32[120,256]{0,1:T(8,128)}, f32[120,256]{0,1:T(8,128)S(1)}, u32[]{:S(2)}, u32[]{:S(2)}) collective-permute-start(f32[120,256]{0,1:T(8,128)} %maximum_maximum_fusion.1), channel_id=1, source_target_pairs={{4,0},{8,4},{12,8},{16,12},{20,16},{24,20},{28,24},{32,28},{36,32}... | collective-permute-start | bytes 368648 | tf_op jit(solution)/shard_map/ppermute | solution.py:18
  20.7 16.2 %copy-start.30 = (s32[1,1,6]{2,1,0:T(1,128)S(1)}, s32[1,1,6]{2,1,0:T(1,128)}, u32[]{:S(2)}) copy-start(s32[1,1,6]{2,1,0:T(1,128)} %param.11) | copy-start | bytes 76
  20.7 18.9 %collective-permute-start = (f32[120,256]{0,1:T(8,128)}, f32[120,256]{0,1:T(8,128)S(1)}, u32[]{:S(2)}, u32[]{:S(2)}) collective-permute-start(f32[120,256]{0,1:T(8,128)} %maximum_maximum_fusion), channel_id=1, source_target_pairs={{0,4},{4,8},{8,12},{12,16},{16,20},{20,24},{24,28},{28,32},{32,36}... | collective-permute-start | bytes 368648 | tf_op jit(solution)/shard_map/ppermute | solution.py:18
  23.6 17.6 %collective-permute-start.2 = (f32[120,256]{0,1:T(8,128)}, f32[120,256]{0,1:T(8,128)S(1)}, u32[]{:S(2)}, u32[]{:S(2)}) collective-permute-start(f32[120,256]{0,1:T(8,128)} %maximum_maximum_fusion.2), channel_id=1, source_target_pairs={{0,64},{4,68},{8,72},{12,76},{16,80},{20,84},{24,88},{28,92},{32,9... | collective-permute-start | bytes 368648 | tf_op jit(solution)/shard_map/ppermute | solution.py:18
  28.7 38.8 %collective-permute-start.3 = (f32[120,256]{0,1:T(8,128)}, f32[120,256]{0,1:T(8,128)}, u32[]{:S(2)}, u32[]{:S(2)}) collective-permute-start(f32[120,256]{0,1:T(8,128)} %maximum_maximum_fusion.3), channel_id=1, source_target_pairs={{64,0},{68,4},{72,8},{76,12},{80,16},{84,20},{88,24},{92,28},{96,3... | collective-permute-start | bytes 368648 | tf_op jit(solution)/shard_map/ppermute | solution.py:18
  30.9 60.8 %copy-start.5 = (f32[1,1,48,192]{2,3,1,0:T(8,128)}, f32[1,1,48,192]{2,3,1,0:T(8,128)S(1)}, u32[]{:S(2)}) copy-start(f32[1,1,48,192]{2,3,1,0:T(8,128)S(1)} %copy.126) | copy-start | bytes 110596
  32.9 35.6 %copy-start.22 = (f32[1,48,96]{1,2,0:T(8,128)S(1)}, f32[1,48,96]{1,2,0:T(8,128)}, u32[]{:S(2)}) copy-start(f32[1,48,96]{1,2,0:T(8,128)} %get-tuple-element.26) | copy-start | bytes 55300
  32.9 42.1 %collective-permute-start.4 = (f32[168,256]{0,1:T(8,128)}, f32[168,256]{0,1:T(8,128)}, u32[]{:S(2)}, u32[]{:S(2)}) collective-permute-start(f32[168,256]{0,1:T(8,128)} %get-tuple-element.53), channel_id=1, source_target_pairs={{0,1},{1,2},{2,3},{4,5},{5,6},{6,7},{8,9},{9,10},{10,11},{12,13},{... | collective-permute-start | bytes 516104 | tf_op jit(solution)/shard_map/ppermute | solution.py:18
  36.9 87.7 %copy-start.26 = (pred[6]{0:T(512)(128)(4,1)}, pred[6]{0:T(512)(128)(4,1)S(1)}, u32[]{:S(2)}) copy-start(pred[6]{0:T(512)(128)(4,1)S(1)} %get-tuple-element.76) | copy-start | bytes 22
  36.9 87.7 %copy-start.28 = (pred[6]{0:T(512)(128)(4,1)}, pred[6]{0:T(512)(128)(4,1)S(1)}, u32[]{:S(2)}) copy-start(pred[6]{0:T(512)(128)(4,1)S(1)} %get-tuple-element.77) | copy-start | bytes 22
  37.6 87.1 %copy-start.24 = (f32[6]{0:T(128)}, f32[6]{0:T(128)S(1)}, u32[]{:S(2)}) copy-start(f32[6]{0:T(128)S(1)} %get-tuple-element.74) | copy-start | bytes 76
  37.6 31.6 %copy-start.21 = (f32[1,48,96]{1,2,0:T(8,128)S(1)}, f32[1,48,96]{1,2,0:T(8,128)}, u32[]{:S(2)}) copy-start(f32[1,48,96]{1,2,0:T(8,128)} %get-tuple-element.25) | copy-start | bytes 55300
  37.7 32.2 %copy-start.20 = (f32[1,48,96]{1,2,0:T(8,128)S(1)}, f32[1,48,96]{1,2,0:T(8,128)}, u32[]{:S(2)}) copy-start(f32[1,48,96]{1,2,0:T(8,128)} %get-tuple-element.28) | copy-start | bytes 55300
  37.7 32.9 %copy-start.19 = (f32[1,48,96]{1,2,0:T(8,128)S(1)}, f32[1,48,96]{1,2,0:T(8,128)}, u32[]{:S(2)}) copy-start(f32[1,48,96]{1,2,0:T(8,128)} %get-tuple-element.27) | copy-start | bytes 55300
  39.5 28.9 %copy-start.15 = (f32[120,256]{0,1:T(8,128)}, f32[120,256]{0,1:T(8,128)S(1)}, u32[]{:S(2)}) copy-start(f32[120,256]{0,1:T(8,128)S(1)} %collective-permute-done) | copy-start | bytes 368644
  39.5 36.4 %collective-permute-start.5 = (f32[168,256]{0,1:T(8,128)}, f32[168,256]{0,1:T(8,128)S(1)}, u32[]{:S(2)}, u32[]{:S(2)}) collective-permute-start(f32[168,256]{0,1:T(8,128)} %get-tuple-element.52), channel_id=1, source_target_pairs={{1,0},{2,1},{3,2},{5,4},{6,5},{7,6},{9,8},{10,9},{11,10},{13,12},{... | collective-permute-start | bytes 516104 | tf_op jit(solution)/shard_map/ppermute | solution.py:18
  40.9 27.5 %copy-start.14 = (f32[120,256]{0,1:T(8,128)}, f32[120,256]{0,1:T(8,128)S(1)}, u32[]{:S(2)}) copy-start(f32[120,256]{0,1:T(8,128)S(1)} %collective-permute-done.1) | copy-start | bytes 368644
  41.1 27.3 %copy-start.16 = (f32[120,256]{0,1:T(8,128)}, f32[120,256]{0,1:T(8,128)S(1)}, u32[]{:S(2)}) copy-start(f32[120,256]{0,1:T(8,128)S(1)} %collective-permute-done.2) | copy-start | bytes 368644
  76.0 4.0 %copy-start.8 = (f32[1,1,576,48]{2,3,1,0:T(8,128)S(1)}, f32[1,1,576,48]{2,3,1,0:T(8,128)}, u32[]{:S(2)}) copy-start(f32[1,1,576,48]{2,3,1,0:T(8,128)} %param.8) | copy-start | bytes 331780
  76.0 0.7 copy-start.13
  79.9 10.6 %copy-start.18 = (f32[1,48,96]{1,2,0:T(8,128)S(1)}, f32[1,48,96]{1,2,0:T(8,128)}, u32[]{:S(2)}) copy-start(f32[1,48,96]{1,2,0:T(8,128)} %get-tuple-element.29) | copy-start | bytes 55300
  81.7 13.2 %copy-start.17 = (f32[1,48,96]{1,2,0:T(8,128)S(1)}, f32[1,48,96]{1,2,0:T(8,128)}, u32[]{:S(2)}) copy-start(f32[1,48,96]{1,2,0:T(8,128)} %get-tuple-element.24) | copy-start | bytes 55300
  82.4 9.2 %all-to-all-start = ((f32[4,48,256]{2,1,0:T(8,128)}), f32[4,48,256]{2,1,0:T(8,128)S(1)}, u32[]{:S(2)}, u32[]{:S(2)}) async-start(f32[4,48,256]{2,1,0:T(8,128)} %broadcast_in_dim.42), calls=%async_computation | async-start | bytes 393216 | tf_op jit(solution)/shard_map/all_to_all | solution.py:38
  89.5 35.1 %copy-start.9 = (f32[48,192]{0,1:T(8,128)}, f32[48,192]{0,1:T(8,128)S(1)}, u32[]{:S(2)}) copy-start(f32[48,192]{0,1:T(8,128)S(1)} %slice.342) | copy-start | bytes 110596
  90.5 34.0 %copy-start.10 = (f32[48,192]{0,1:T(8,128)}, f32[48,192]{0,1:T(8,128)S(1)}, u32[]{:S(2)}) copy-start(f32[48,192]{0,1:T(8,128)S(1)} %slice.343) | copy-start | bytes 110596
  92.3 20.0 %collective-permute-start.6 = (f32[48,256]{1,0:T(8,128)S(1)}, f32[48,256]{1,0:T(8,128)S(1)}, u32[]{:S(2)}, u32[]{:S(2)}) collective-permute-start(f32[48,256]{1,0:T(8,128)S(1)} %get-tuple-element.43), channel_id=1, source_target_pairs={{0,4},{4,8},{8,12},{12,16},{16,20},{20,24},{24,28},{28,32},{32,36}... | collective-permute-start | bytes 147464 | tf_op jit(solution)/shard_map/ppermute | solution.py:18
  95.6 32.7 %copy-start.6 = (f32[6,96,96]{1,2,0:T(8,128)}, f32[6,96,96]{1,2,0:T(8,128)S(1)}, u32[]{:S(2)}) copy-start(f32[6,96,96]{1,2,0:T(8,128)S(1)} %constant_dynamic-update-slice_fusion) | copy-start | bytes 663556
  95.6 16.7 %collective-permute-start.7 = (f32[48,256]{1,0:T(8,128)S(1)}, f32[48,256]{1,0:T(8,128)S(1)}, u32[]{:S(2)}, u32[]{:S(2)}) collective-permute-start(f32[48,256]{1,0:T(8,128)S(1)} %get-tuple-element.43), channel_id=1, source_target_pairs={{4,0},{8,4},{12,8},{16,12},{20,16},{24,20},{28,24},{32,28},{36,32}... | collective-permute-start | bytes 147464 | tf_op jit(solution)/shard_map/ppermute | solution.py:18
  98.1 14.3 %collective-permute-start.8 = (f32[48,256]{1,0:T(8,128)S(1)}, f32[48,256]{1,0:T(8,128)S(1)}, u32[]{:S(2)}, u32[]{:S(2)}) collective-permute-start(f32[48,256]{1,0:T(8,128)S(1)} %get-tuple-element.43), channel_id=1, source_target_pairs={{0,64},{4,68},{8,72},{12,76},{16,80},{20,84},{24,88},{28,92},{32,9... | collective-permute-start | bytes 147464 | tf_op jit(solution)/shard_map/ppermute | solution.py:18
  111.0 13.5 %collective-permute-start.9 = (f32[48,256]{1,0:T(8,128)S(1)}, f32[48,256]{1,0:T(8,128)S(1)}, u32[]{:S(2)}, u32[]{:S(2)}) collective-permute-start(f32[48,256]{1,0:T(8,128)S(1)} %get-tuple-element.43), channel_id=1, source_target_pairs={{64,0},{68,4},{72,8},{76,12},{80,16},{84,20},{88,24},{92,28},{96,3... | collective-permute-start | bytes 147464 | tf_op jit(solution)/shard_map/ppermute | solution.py:18
  133.2 17.7 %collective-permute-start.10 = (f32[96,256]{0,1:T(8,128)S(1)}, f32[96,256]{0,1:T(8,128)S(1)}, u32[]{:S(2)}, u32[]{:S(2)}) collective-permute-start(f32[96,256]{0,1:T(8,128)S(1)} %get-tuple-element.17), channel_id=1, source_target_pairs={{0,4},{4,8},{8,12},{12,16},{16,20},{20,24},{24,28},{28,32},{32,36}... | collective-permute-start | bytes 294920 | tf_op jit(solution)/shard_map/ppermute | solution.py:18
  136.7 16.3 %collective-permute-start.11 = (f32[96,256]{0,1:T(8,128)S(1)}, f32[96,256]{0,1:T(8,128)S(1)}, u32[]{:S(2)}, u32[]{:S(2)}) collective-permute-start(f32[96,256]{0,1:T(8,128)S(1)} %get-tuple-element.16), channel_id=1, source_target_pairs={{4,0},{8,4},{12,8},{16,12},{20,16},{24,20},{28,24},{32,28},{36,32}... | collective-permute-start | bytes 294920 | tf_op jit(solution)/shard_map/ppermute | solution.py:18
  140.9 21.5 %collective-permute-start.12 = (f32[96,256]{0,1:T(8,128)S(1)}, f32[96,256]{0,1:T(8,128)S(1)}, u32[]{:S(2)}, u32[]{:S(2)}) collective-permute-start(f32[96,256]{0,1:T(8,128)S(1)} %get-tuple-element.15), channel_id=1, source_target_pairs={{0,64},{4,68},{8,72},{12,76},{16,80},{20,84},{24,88},{28,92},{32,9... | collective-permute-start | bytes 294920 | tf_op jit(solution)/shard_map/ppermute | solution.py:18
  147.5 23.6 %collective-permute-start.13 = (f32[96,256]{0,1:T(8,128)S(1)}, f32[96,256]{0,1:T(8,128)S(1)}, u32[]{:S(2)}, u32[]{:S(2)}) collective-permute-start(f32[96,256]{0,1:T(8,128)S(1)} %get-tuple-element.14), channel_id=1, source_target_pairs={{64,0},{68,4},{72,8},{76,12},{80,16},{84,20},{88,24},{92,28},{96,3... | collective-permute-start | bytes 294920 | tf_op jit(solution)/shard_map/ppermute | solution.py:18
  148.8 22.9 %collective-permute-start.14 = (f32[96,256]{0,1:T(8,128)S(1)}, f32[96,256]{0,1:T(8,128)S(1)}, u32[]{:S(2)}, u32[]{:S(2)}) collective-permute-start(f32[96,256]{0,1:T(8,128)S(1)} %get-tuple-element.13), channel_id=1, source_target_pairs={{0,1},{1,2},{2,3},{4,5},{5,6},{6,7},{8,9},{9,10},{10,11},{12,13},{... | collective-permute-start | bytes 294920 | tf_op jit(solution)/shard_map/ppermute | solution.py:18
  151.0 21.4 %collective-permute-start.15 = (f32[96,256]{0,1:T(8,128)S(1)}, f32[96,256]{0,1:T(8,128)S(1)}, u32[]{:S(2)}, u32[]{:S(2)}) collective-permute-start(f32[96,256]{0,1:T(8,128)S(1)} %get-tuple-element.12), channel_id=1, source_target_pairs={{1,0},{2,1},{3,2},{5,4},{6,5},{7,6},{9,8},{10,9},{11,10},{13,12},{... | collective-permute-start | bytes 294920 | tf_op jit(solution)/shard_map/ppermute | solution.py:18
  178.1 9.4 %all-to-all-start.1 = ((f32[4,48,256]{2,1,0:T(8,128)}), f32[4,48,256]{2,1,0:T(8,128)}, u32[]{:S(2)}, u32[]{:S(2)}) async-start(f32[4,48,256]{2,1,0:T(8,128)} %broadcast_in_dim.44), calls=%async_computation.1 | async-start | bytes 393216 | tf_op jit(solution)/shard_map/all_to_all | solution.py:38
  189.2 0.7 copy-start.11
  189.9 20.8 %collective-permute-start.16 = (f32[48,256]{1,0:T(8,128)S(1)}, f32[48,256]{1,0:T(8,128)}, u32[]{:S(2)}, u32[]{:S(2)}) collective-permute-start(f32[48,256]{1,0:T(8,128)S(1)} %get-tuple-element.41), channel_id=1, source_target_pairs={{0,4},{4,8},{8,12},{12,16},{16,20},{20,24},{24,28},{28,32},{32,36}... | collective-permute-start | bytes 147464 | tf_op jit(solution)/shard_map/ppermute | solution.py:18
  194.4 1.2 copy-start.4
  195.6 28.3 %copy-start.12 = (f32[144,256]{1,0:T(8,128)S(1)}, f32[144,256]{1,0:T(8,128)}, u32[]{:S(2)}) copy-start(f32[144,256]{1,0:T(8,128)} %copy-done.11) | copy-start | bytes 442372
  195.6 28.3 %copy-start.23 = (f32[48,256]{1,0:T(8,128)S(1)}, f32[48,256]{1,0:T(8,128)}, u32[]{:S(2)}) copy-start(f32[48,256]{1,0:T(8,128)} %get-tuple-element.40) | copy-start | bytes 147460
  195.6 28.3 %copy-start.7 = (f32[6,96,96]{1,2,0:T(8,128)S(1)}, f32[6,96,96]{1,2,0:T(8,128)}, u32[]{:S(2)}) copy-start(f32[6,96,96]{1,2,0:T(8,128)} %copy-done.6) | copy-start | bytes 663556
  195.6 28.3 %copy-start.25 = (f32[6]{0:T(128)S(1)}, f32[6]{0:T(128)}, u32[]{:S(2)}) copy-start(f32[6]{0:T(128)} %copy-done.24) | copy-start | bytes 76
  196.8 27.2 %copy-start.1 = (f32[6,96,256]{1,2,0:T(8,128)S(1)}, f32[6,96,256]{1,2,0:T(8,128)}, u32[]{:S(2)}) copy-start(f32[6,96,256]{1,2,0:T(8,128)} %copy.138) | copy-start | bytes 1769476
  196.8 14.8 %collective-permute-start.17 = (f32[48,256]{1,0:T(8,128)S(1)}, f32[48,256]{1,0:T(8,128)S(1)}, u32[]{:S(2)}, u32[]{:S(2)}) collective-permute-start(f32[48,256]{1,0:T(8,128)S(1)} %get-tuple-element.41), channel_id=1, source_target_pairs={{4,0},{8,4},{12,8},{16,12},{20,16},{24,20},{28,24},{32,28},{36,32}... | collective-permute-start | bytes 147464 | tf_op jit(solution)/shard_map/ppermute | solution.py:18
  200.3 11.2 %collective-permute-start.18 = (f32[48,256]{1,0:T(8,128)S(1)}, f32[48,256]{1,0:T(8,128)S(1)}, u32[]{:S(2)}, u32[]{:S(2)}) collective-permute-start(f32[48,256]{1,0:T(8,128)S(1)} %get-tuple-element.41), channel_id=1, source_target_pairs={{0,64},{4,68},{8,72},{12,76},{16,80},{20,84},{24,88},{28,92},{32,9... | collective-permute-start | bytes 147464 | tf_op jit(solution)/shard_map/ppermute | solution.py:18
  209.4 14.4 %collective-permute-start.19 = (f32[48,256]{1,0:T(8,128)S(1)}, f32[48,256]{1,0:T(8,128)S(1)}, u32[]{:S(2)}, u32[]{:S(2)}) collective-permute-start(f32[48,256]{1,0:T(8,128)S(1)} %get-tuple-element.41), channel_id=1, source_target_pairs={{64,0},{68,4},{72,8},{76,12},{80,16},{84,20},{88,24},{92,28},{96,3... | collective-permute-start | bytes 147464 | tf_op jit(solution)/shard_map/ppermute | solution.py:18
  233.4 72.0 %copy-start.27 = (pred[6]{0:T(512)(128)(4,1)S(1)}, pred[6]{0:T(512)(128)(4,1)}, u32[]{:S(2)}) copy-start(pred[6]{0:T(512)(128)(4,1)} %copy-done.26) | copy-start | bytes 22
  233.4 72.0 %copy-start.29 = (pred[6]{0:T(512)(128)(4,1)S(1)}, pred[6]{0:T(512)(128)(4,1)}, u32[]{:S(2)}) copy-start(pred[6]{0:T(512)(128)(4,1)} %copy-done.28) | copy-start | bytes 22
  307.0 2.3 copy-start.2

commit v3 on v2

v3 whole, which is shorter than its diff:
```python
import functools

import jax
import jax.numpy as jnp
from jax import lax
from jax.experimental import pallas as pl
from jax.experimental.pallas import tpu as pltpu
from jax.sharding import Mesh, PartitionSpec as P


SUBROW = 16
SLOTS = 6
LANES = 128
PLANE = ("y", "core", "grp")
SUB = ("y", "z", "core")
SOURCES = ((SUB, -1), (SUB, 1), (SUB, -SUBROW), (SUB, SUBROW), ("grp", -1), ("grp", 1))
ORDER = (2, 3, 0, 1, 4, 5)


def fetch(piece, slot):
    axis, offset = SOURCES[slot]
    count = lax.axis_size(axis)
    pairs = [(i, i - offset) for i in range(count) if 0 <= i - offset < count]
    return lax.ppermute(piece, axis, pairs)


def exchange(pieces):
    gotten = [None] * len(pieces)
    for slot in ORDER:
        if slot < len(pieces):
            gotten[slot] = fetch(pieces[slot], slot)
    return gotten


def swap(blocks, axes):
    return lax.all_to_all(blocks, axes, 0, 0, tiled=True)


def total(terms):
    plane = lax.axis_size(PLANE)
    chunks = terms.reshape(plane, -1)
    chunk = jnp.sum(swap(chunks, PLANE), axis=0)
    chunk = jnp.sum(swap(jnp.broadcast_to(chunk, (lax.axis_size("z"),) + chunk.shape), "z"), axis=0)
    return swap(jnp.broadcast_to(chunk, chunks.shape), PLANE).reshape(terms.shape)


def dot(left, right, across=1):
    return lax.dot_general(
        left, right, (((across,), (0,)), ((), ())),
        precision=lax.Precision.HIGHEST, preferred_element_type=jnp.float32,
    )


def clamp(values, slot, touching):
    bounded = jnp.maximum(values, 0.0) if slot % 2 else jnp.minimum(values, 0.0)
    return jnp.where(touching, bounded, values)


def kernel_call(body, flags, arrays, outs, flops):
    smem = pl.BlockSpec(memory_space=pltpu.SMEM)
    vmem = pl.BlockSpec(memory_space=pltpu.VMEM)
    moved = sum(a.size for a in arrays) + sum(o[0] * o[1] if len(o) == 2 else o[0] * o[1] * o[2] for o in outs)
    return pl.pallas_call(
        functools.partial(body, len(flags), len(arrays)),
        out_shape=[jax.ShapeDtypeStruct(o, jnp.float32) for o in outs],
        in_specs=[smem] * len(flags) + [vmem] * len(arrays),
        out_specs=[vmem] * len(outs),
        compiler_params=pltpu.CompilerParams(vmem_limit_bytes=24 << 20),
        cost_estimate=pl.CostEstimate(flops=flops, bytes_accessed=4 * moved, transcendentals=0),
    )(*flags, *arrays)


def split(refs, flags, arrays):
    return refs[:flags], refs[flags:flags + arrays], refs[flags + arrays:]


def pack_kernel(nf, na, *refs):
    _, (gap, shapes, rows), outs = split(refs, nf, na)
    face = gap.shape[0] // SLOTS
    half = shapes.shape[0] // 2
    for slot, out in enumerate(outs):
        at = (slot ^ 1) * face
        out[:face] = gap[at:at + face]
        piece = shapes[:, at:at + face]
        out[face:face + half] = jnp.zeros((half, out.shape[1]), jnp.float32)
        out[face:face + half, :face] = piece[:half]
        out[face:face + half, LANES:LANES + face] = piece[half:]
        if slot >= 4:
            out[face + half:] = jnp.zeros((2 * half, out.shape[1]), jnp.float32)
            out[face + half:, :rows.shape[1]] = rows[...]


def residual_kernel(sign, nf, na, *refs):
    (live,), (own, shapes, *gotten), (values, spread) = split(refs, nf, na)
    face = values.shape[0] // SLOTS
    for slot in range(SLOTS):
        at = slot * face
        gap = own[at:at + face] if own.shape[0] == values.shape[0] else None
        values[at:at + face] = live[0, slot].astype(jnp.float32) * (sign * (gap - gotten[slot][:face]))
    coef = dot(shapes[...], values[...])
    for row in range(spread.shape[0]):
        spread[row] = coef


def coarse_kernel(nf, na, *refs):
    _, (rows, coefs), (own,) = split(refs, nf, na)
    own[...] = dot(rows[...], coefs[...])


def corrected(live, values, shapes, own, coefs, near, messages):
    face = values.shape[0] // SLOTS
    kinds = shapes.shape[0]
    half = kinds // 2
    mine = dot(shapes[...].T, own[...])
    faces = []
    for slot in range(SLOTS):
        at = slot * face
        message = messages[slot]
        if slot < 4:
            other = near[slot][...]
        else:
            other = dot(message[face + half:, :coefs.shape[0]], coefs[...])
        packed = message[face:face + half]
        theirs = dot(jnp.concatenate([packed[:, :face], packed[:, LANES:LANES + face]]).T, other)
        keep = live[0, slot].astype(jnp.float32)
        faces.append(values[at:at + face] - keep * (mine[at:at + face] - theirs))
    return faces


def push_kernel(nf, na, *refs):
    (live, contact), (values, operator, shapes, own, coefs, *rest), (first, push, *pushed) = split(refs, nf, na)
    near, messages = rest[:4], rest[4:]
    face = values.shape[0] // SLOTS
    for slot, part in enumerate(corrected(live, values, shapes, own, coefs, near, messages)):
        at = slot * face
        first[at:at + face] = part
        push[at:at + face] = clamp(-part, slot, contact[0, slot] > 0)
    for slot in range(SLOTS):
        at = slot * face
        pushed[slot][...] = dot(operator[at:at + face], push[...])


def image_kernel(nf, na, *refs):
    _, (operator, first), (image,) = split(refs, nf, na)
    image[...] = dot(operator[...], first[...])


def change_kernel(nf, na, *refs):
    (live,), (values, operator, shapes, first, image, own, coefs, *rest), (change, sums) = split(refs, nf, na)
    near, messages = rest[:4], rest[4:]
    face = values.shape[0] // SLOTS
    for slot, part in enumerate(corrected(live, values, shapes, own, coefs, near, messages)):
        change[slot * face:(slot + 1) * face] = part
    moved = dot(operator[...], change[...])

    def inner(left, right):
        return jnp.sum(left * right, axis=0, keepdims=True)

    sums[0:1] = inner(first[...], first[...])
    sums[1:2] = inner(first[...], image[...])
    sums[2:3] = inner(first[...], change[...])
    sums[3:4] = inner(change[...], change[...])
    sums[4:5] = inner(change[...], image[...])
    sums[5:6] = inner(change[...], moved)


def finish_kernel(nf, na, *refs):
    (contact,), (sums, first, push, change), (multipliers, direction) = split(refs, nf, na)
    face = first.shape[0] // SLOTS
    s = [sums[i:i + 1] for i in range(6)]
    step = s[0] / (2.0 * s[1])
    norm = s[0] + step * (2.0 * s[2] + step * s[3])
    curvature = 2.0 * (s[1] + step * (2.0 * s[4] + step * s[5]))
    ratio = norm / curvature
    for slot in range(SLOTS):
        rows = slice(slot * face, (slot + 1) * face)
        part = first[rows] + step * change[rows]
        direction[rows] = part
        multipliers[rows] = clamp(step * push[rows] - ratio * part, slot, contact[0, slot] > 0)


def opened(nf, na, *refs):
    (live,), (shapes, *faces), (values, spread) = split(refs, nf, na)
    pushed, gotten = faces[:SLOTS], faces[SLOTS:]
    face = values.shape[0] // SLOTS
    for slot in range(SLOTS):
        at = slot * face
        values[at:at + face] = live[0, slot].astype(jnp.float32) * (pushed[slot][...] - gotten[slot][...])
    coef = dot(shapes[...], values[...])
    for row in range(spread.shape[0]):
        spread[row] = coef


def body(dual_ops, gap_parts, modes, coarse_rows, face_live, contact):
    operator = dual_ops[0, 0]
    dual_rows = operator.shape[0]
    face = dual_rows // SLOTS
    cases = gap_parts.shape[3]
    kinds = modes.shape[3]
    groups = lax.axis_size("grp")
    live, touching = face_live[0], contact[0]
    rows = coarse_rows[0, 0]
    parts = gap_parts[0, 0]
    shapes = modes[0, 0].T
    short, long = face + kinds // 2, face + kinds // 2 + kinds
    whole = (dual_rows, cases)
    spread = (groups, kinds, cases)
    heavy = 12 * dual_rows * dual_rows * cases
    light = 12 * dual_rows * kinds * cases

    messages = kernel_call(
        pack_kernel, [], [parts, shapes, rows],
        [(short if slot < 4 else long, cases) for slot in range(SLOTS)], 0,
    )
    messages = exchange(messages)

    def coarse(spread_coef):
        coefs = swap(spread_coef, "grp").reshape(groups * kinds, cases)
        own, = kernel_call(coarse_kernel, [], [rows, coefs], [(kinds, cases)], light // 3)
        return own, coefs, exchange([own] * 4)

    values, coef = kernel_call(
        functools.partial(residual_kernel, -1.0), [live], [parts, shapes, *messages], [whole, spread], light
    )
    own, coefs, near = coarse(coef)
    first, push, *pushed = kernel_call(
        push_kernel, [live, touching], [values, operator, shapes, own, coefs, *near, *messages],
        [whole, whole] + [(face, cases)] * SLOTS, heavy + 2 * light,
    )
    gotten = exchange([pushed[slot ^ 1] for slot in range(SLOTS)])
    image, = kernel_call(image_kernel, [], [operator, first], [whole], heavy)
    values, coef = kernel_call(opened, [live], [shapes, *pushed, *gotten], [whole, spread], light)
    own, coefs, near = coarse(coef)
    change, sums = kernel_call(
        change_kernel, [live], [values, operator, shapes, first, image, own, coefs, *near, *messages],
        [whole, (6, cases)], heavy + 2 * light,
    )
    multipliers, direction = kernel_call(
        finish_kernel, [touching], [total(sums), first, push, change], [whole, whole], 8 * dual_rows * cases
    )
    shape = (1, 1) + whole
    return (multipliers.reshape(shape), direction.reshape(shape))


def solution(mesh):
    fine = Mesh(mesh.devices.reshape(4, 32, 2, 4), ("y", "z", "core", "grp"))
    wide = P(SUB, "grp", None, None)
    flags = P(SUB, "grp", None)
    return jax.shard_map(
        body, mesh=fine, in_specs=(wide, wide, wide, wide, flags, flags), out_specs=(wide, wide), check_vma=False
    )
```

time: 312 us -> 262 us (0.84)
  local copies, waits for them, and re-layouts: 40.3 us -> 4.12 us
  matrix products: 21.5 us -> 0 us
  blocking collectives: 68.5 us -> 87.3 us
  Pallas kernels: 0 us -> 14.2 us
  other arithmetic: 14.6 us -> 0.76 us
  starting transfers between devices: 91.1 us -> 83.2 us
    dot_general x9 -> x0, matrix products: 21.5 us -> none  [the longest x7 15.1 us: matmul(): jnp.dot(left, right, precision=lax.Precision.HIGHEST, preferred_element_t...]
    all_to_all x3 -> x5, blocking collectives: 68.5 us -> 87.3 us  [swap(): return lax.all_to_all(blocks, axes, 0, 0, tiled=True)]
    pallas_call x0 -> x9, Pallas kernels: none -> 14.2 us  [kernel_call(): pl.pallas_call(functools.partial(body, len(flags), len(arrays)), out_shap...]
    all_to_all x2 -> x0, starting transfers between devices: 8.19 us -> none  [swap(): return lax.all_to_all(blocks, axes, 0, 0, tiled=True)]
    slice x15 -> x0, local copies, waits for them, and re-layouts: 7.72 us -> none  [the longest x6 2.96 us: body(): packed[:, :face_rows]]
    another operation x8 -> x0, local copies, waits for them, and re-layouts: 7.55 us -> none  [the longest x3 3.23 us: body(): parts_across = jnp.stack([message[:face_rows] for message in gotten])]
    unnamed x76 -> x16, local copies, waits for them, and re-layouts: 9.83 us -> 3.43 us
    all_to_all x2 -> x0, waiting for transfers between devices: 5.41 us -> none  [swap(): return lax.all_to_all(blocks, axes, 0, 0, tiled=True)]
  transfers between devices with their start and end apart: 22 -> 20, of which waited for: 7 -> 6; matrix products, arithmetic and copies ran while one was open for 10% -> 0% of each run, Pallas kernels for 0% -> 1%
where the time goes in v3:
time: 262 us; the launch traced here: 261 us
  blocking collectives  87.3 us (33%)
  starting transfers between devices  83.2 us (32%)
  waiting for transfers between devices  70.4 us (27%)
  Pallas kernels  14.2 us (5%)
  local copies, waits for them, and re-layouts  4.12 us (2%)
    all_to_all x5, blocking collectives, swap(): return lax.all_to_all(blocks, axes, 0, 0, tiled=True)  87.3 us
    ppermute x20, starting transfers between devices, fetch(): return lax.ppermute(piece, axis, pairs)  83.2 us
    ppermute x20, waiting for transfers between devices, fetch(): return lax.ppermute(piece, axis, pairs)  70.4 us
    pallas_call x9, Pallas kernels, kernel_call(): pl.pallas_call(functools.partial(body, len(flags), len(arrays)), out_shap...  14.2 us
  transfers between devices with their start and end apart: 20, of which 6 were waited for; matrix products, arithmetic and copies ran while one was open for 0% of the time, Pallas kernels for 1%

profile of v3, /device:TPU:1, one launch (start us, length us, event | category | flops | bytes accessed | tf_op | source)
XLA Modules:
  0.0 261.0 jit_solution(7049575007375718716)
XLA Ops:
  0.6 0.0 copy-start.7
  0.7 1.1 copy-done
  1.7 0.9 copy-done.1
  2.6 0.8 copy-done.4
  3.4 0.1 shard_map.77
  3.5 5.1 %collective-permute-start = (f32[120,256]{1,0:T(8,128)S(1)}, f32[120,256]{1,0:T(8,128)S(1)}, u32[]{:S(2)}, u32[]{:S(2)}) collective-permute-start(f32[120,256]{1,0:T(8,128)S(1)} %get-tuple-element.24), channel_id=1, source_target_pairs={{0,4},{4,8},{8,12},{12,16},{16,20},{20,24},{24,28},{28,32},{32,36}... | collective-permute-start | bytes 368648 | tf_op jit(solution)/shard_map/ppermute | solution.py:24
  8.6 3.1 %collective-permute-start.4 = (f32[168,256]{1,0:T(8,128)S(1)}, f32[168,256]{1,0:T(8,128)S(1)}, u32[]{:S(2)}, u32[]{:S(2)}) collective-permute-start(f32[168,256]{1,0:T(8,128)S(1)} %get-tuple-element.28), channel_id=1, source_target_pairs={{0,1},{1,2},{2,3},{4,5},{5,6},{6,7},{8,9},{9,10},{10,11},{12,13},{... | collective-permute-start | bytes 516104 | tf_op jit(solution)/shard_map/ppermute | solution.py:24
  11.7 1.3 collective-permute-start.5
  13.0 10.6 %collective-permute-start.1 = (f32[120,256]{1,0:T(8,128)S(1)}, f32[120,256]{1,0:T(8,128)S(1)}, u32[]{:S(2)}, u32[]{:S(2)}) collective-permute-start(f32[120,256]{1,0:T(8,128)S(1)} %get-tuple-element.25), channel_id=1, source_target_pairs={{4,0},{8,4},{12,8},{16,12},{20,16},{24,20},{28,24},{32,28},{36,32}... | collective-permute-start | bytes 368648 | tf_op jit(solution)/shard_map/ppermute | solution.py:24
  23.6 6.8 %collective-permute-start.2 = (f32[120,256]{1,0:T(8,128)S(1)}, f32[120,256]{1,0:T(8,128)S(1)}, u32[]{:S(2)}, u32[]{:S(2)}) collective-permute-start(f32[120,256]{1,0:T(8,128)S(1)} %get-tuple-element.26), channel_id=1, source_target_pairs={{0,64},{4,68},{8,72},{12,76},{16,80},{20,84},{24,88},{28,92},{32,9... | collective-permute-start | bytes 368648 | tf_op jit(solution)/shard_map/ppermute | solution.py:24
  30.4 0.0 collective-permute-done.refs_3_.refs_11_.refs_12_
  30.4 1.3 collective-permute-start.3
  31.7 0.0 collective-permute-done.1.refs_4_.refs_12_.refs_13_
  31.7 0.5 collective-permute-done.2.refs_5_.refs_13_.refs_14_
  32.3 34.5 %collective-permute-done.3.refs_6_.refs_14_.refs_15_ = f32[120,256]{1,0:T(8,128)S(1)} collective-permute-done((f32[120,256]{1,0:T(8,128)S(1)}, f32[120,256]{1,0:T(8,128)S(1)}, u32[]{:S(2)}, u32[]{:S(2)}) %collective-permute-start.3) | collective-permute-done | bytes 122912 | tf_op jit(solution)/shard_map/ppermute | solution.py:24
  66.7 0.0 collective-permute-done.4.refs_7_.refs_15_.refs_16_
  66.7 0.0 collective-permute-done.5.refs_8_.refs_16_.refs_17_
  66.7 0.7 copy-done.6
  67.4 1.1 shard_map.78
  68.5 9.9 %all_to_all.31 = f32[4,48,256]{2,1,0:T(8,128)S(1)} all-to-all(f32[4,48,256]{2,1,0:T(8,128)S(1)} %get-tuple-element.31), channel_id=1, replica_groups=mesh['y'=4,'z'=32,'core'=2,'grp'=4] {'grp'}, dimensions={0} | all-to-all | bytes 393216 | tf_op jit(solution)/shard_map/all_to_all | solution.py:36
  78.3 0.2 shard_map.79.refs_5_
  78.5 3.3 %collective-permute-start.6 = (f32[48,256]{1,0:T(8,128)S(1)}, f32[48,256]{1,0:T(8,128)S(1)}, u32[]{:S(2)}, u32[]{:S(2)}) collective-permute-start(f32[48,256]{1,0:T(8,128)S(1)} %shard_map.79.refs_5_), channel_id=1, source_target_pairs={{0,4},{4,8},{8,12},{12,16},{16,20},{20,24},{24,28},{28,32},{32,36}... | collective-permute-start | bytes 147464 | tf_op jit(solution)/shard_map/ppermute | solution.py:24
  81.9 2.2 collective-permute-start.7
  84.1 12.7 %collective-permute-start.8 = (f32[48,256]{1,0:T(8,128)S(1)}, f32[48,256]{1,0:T(8,128)S(1)}, u32[]{:S(2)}, u32[]{:S(2)}) collective-permute-start(f32[48,256]{1,0:T(8,128)S(1)} %shard_map.79.refs_5_), channel_id=1, source_target_pairs={{0,64},{4,68},{8,72},{12,76},{16,80},{20,84},{24,88},{28,92},{32,9... | collective-permute-start | bytes 147464 | tf_op jit(solution)/shard_map/ppermute | solution.py:24
  96.8 1.3 collective-permute-start.9
  98.1 0.0 collective-permute-done.6.refs_7_
  98.1 0.0 collective-permute-done.7.refs_8_
  98.2 0.0 collective-permute-done.8.refs_9_
  98.2 12.3 %collective-permute-done.9.refs_10_ = f32[48,256]{1,0:T(8,128)S(1)} collective-permute-done((f32[48,256]{1,0:T(8,128)S(1)}, f32[48,256]{1,0:T(8,128)S(1)}, u32[]{:S(2)}, u32[]{:S(2)}) %collective-permute-start.9) | collective-permute-done | bytes 49184 | tf_op jit(solution)/shard_map/ppermute | solution.py:24
  110.5 4.4 %shard_map.80 = (f32[576,256]{1,0:T(8,128)S(1)}, f32[576,256]{1,0:T(8,128)S(1)}, f32[96,256]{1,0:T(8,128)S(1)}, f32[96,256]{1,0:T(8,128)S(1)}, f32[96,256]{1,0:T...) custom-call(s32[1,6]{1,0:T(1,128)S(1)} %bitcast.32, s32[1,6]{1,0:T(1,128)S(1)} %bitcast.35, ...), custom_call_target="tpu_custom_call" | custom-call | flops 1189085184 | bytes 5074944 | tf_op jit(solution)/shard_map/pallas_call | solution.py:63
  114.9 3.5 %collective-permute-start.10 = (f32[96,256]{1,0:T(8,128)S(1)}, f32[96,256]{1,0:T(8,128)S(1)}, u32[]{:S(2)}, u32[]{:S(2)}) collective-permute-start(f32[96,256]{1,0:T(8,128)S(1)} %get-tuple-element.33.refs_3_), channel_id=1, source_target_pairs={{0,4},{4,8},{8,12},{12,16},{16,20},{20,24},{24,28},{28,32},{32,36}... | collective-permute-start | bytes 294920 | tf_op jit(solution)/shard_map/ppermute | solution.py:24
  118.4 4.0 %collective-permute-start.11 = (f32[96,256]{1,0:T(8,128)S(1)}, f32[96,256]{1,0:T(8,128)S(1)}, u32[]{:S(2)}, u32[]{:S(2)}) collective-permute-start(f32[96,256]{1,0:T(8,128)S(1)} %get-tuple-element.32.refs_2_), channel_id=1, source_target_pairs={{4,0},{8,4},{12,8},{16,12},{20,16},{24,20},{28,24},{32,28},{36,32}... | collective-permute-start | bytes 294920 | tf_op jit(solution)/shard_map/ppermute | solution.py:24
  122.4 6.8 %collective-permute-start.12 = (f32[96,256]{1,0:T(8,128)S(1)}, f32[96,256]{1,0:T(8,128)S(1)}, u32[]{:S(2)}, u32[]{:S(2)}) collective-permute-start(f32[96,256]{1,0:T(8,128)S(1)} %get-tuple-element.35.refs_5_), channel_id=1, source_target_pairs={{0,64},{4,68},{8,72},{12,76},{16,80},{20,84},{24,88},{28,92},{32,9... | collective-permute-start | bytes 294920 | tf_op jit(solution)/shard_map/ppermute | solution.py:24
  129.2 1.3 collective-permute-start.13
  130.5 2.2 collective-permute-start.14
  132.7 0.0 collective-permute-done.10.refs_8_
  132.7 1.3 collective-permute-start.15
  134.0 0.0 collective-permute-done.11.refs_9_
  134.0 3.2 %collective-permute-done.12.refs_10_ = f32[96,256]{1,0:T(8,128)S(1)} collective-permute-done((f32[96,256]{1,0:T(8,128)S(1)}, f32[96,256]{1,0:T(8,128)S(1)}, u32[]{:S(2)}, u32[]{:S(2)}) %collective-permute-start.12) | collective-permute-done | bytes 98336 | tf_op jit(solution)/shard_map/ppermute | solution.py:24
  137.2 9.3 %collective-permute-done.13.refs_11_ = f32[96,256]{1,0:T(8,128)S(1)} collective-permute-done((f32[96,256]{1,0:T(8,128)S(1)}, f32[96,256]{1,0:T(8,128)S(1)}, u32[]{:S(2)}, u32[]{:S(2)}) %collective-permute-start.13) | collective-permute-done | bytes 98336 | tf_op jit(solution)/shard_map/ppermute | solution.py:24
  146.5 0.0 collective-permute-done.14.refs_12_
  146.5 0.0 collective-permute-done.15.refs_13_
  146.5 1.0 shard_map.81
  147.6 7.5 %all_to_all.32 = f32[4,48,256]{2,1,0:T(8,128)S(1)} all-to-all(f32[4,48,256]{2,1,0:T(8,128)S(1)} %get-tuple-element.40), channel_id=1, replica_groups=mesh['y'=4,'z'=32,'core'=2,'grp'=4] {'grp'}, dimensions={0} | all-to-all | bytes 393216 | tf_op jit(solution)/shard_map/all_to_all | solution.py:36
  155.1 0.2 shard_map.83.refs_6_
  155.3 2.6 %collective-permute-start.16 = (f32[48,256]{1,0:T(8,128)S(1)}, f32[48,256]{1,0:T(8,128)S(1)}, u32[]{:S(2)}, u32[]{:S(2)}) collective-permute-start(f32[48,256]{1,0:T(8,128)S(1)} %shard_map.83.refs_6_), channel_id=1, source_target_pairs={{0,4},{4,8},{8,12},{12,16},{16,20},{20,24},{24,28},{28,32},{32,36}... | collective-permute-start | bytes 147464 | tf_op jit(solution)/shard_map/ppermute | solution.py:24
  158.0 3.0 %collective-permute-start.17 = (f32[48,256]{1,0:T(8,128)S(1)}, f32[48,256]{1,0:T(8,128)S(1)}, u32[]{:S(2)}, u32[]{:S(2)}) collective-permute-start(f32[48,256]{1,0:T(8,128)S(1)} %shard_map.83.refs_6_), channel_id=1, source_target_pairs={{4,0},{8,4},{12,8},{16,12},{20,16},{24,20},{28,24},{32,28},{36,32}... | collective-permute-start | bytes 147464 | tf_op jit(solution)/shard_map/ppermute | solution.py:24
  161.0 9.5 %collective-permute-start.18 = (f32[48,256]{1,0:T(8,128)S(1)}, f32[48,256]{1,0:T(8,128)S(1)}, u32[]{:S(2)}, u32[]{:S(2)}) collective-permute-start(f32[48,256]{1,0:T(8,128)S(1)} %shard_map.83.refs_6_), channel_id=1, source_target_pairs={{0,64},{4,68},{8,72},{12,76},{16,80},{20,84},{24,88},{28,92},{32,9... | collective-permute-start | bytes 147464 | tf_op jit(solution)/shard_map/ppermute | solution.py:24
  170.5 1.3 collective-permute-start.19
  171.8 1.6 shard_map.82.refs_5_
  173.4 0.0 collective-permute-done.16.refs_8_
  173.4 0.0 collective-permute-done.17.refs_9_
  173.4 0.0 collective-permute-done.18.refs_10_
  173.4 10.6 %collective-permute-done.19.refs_11_ = f32[48,256]{1,0:T(8,128)S(1)} collective-permute-done((f32[48,256]{1,0:T(8,128)S(1)}, f32[48,256]{1,0:T(8,128)S(1)}, u32[]{:S(2)}, u32[]{:S(2)}) %collective-permute-start.19) | collective-permute-done | bytes 49184 | tf_op jit(solution)/shard_map/ppermute | solution.py:24
  184.0 3.9 %shard_map.84 = (f32[576,256]{1,0:T(8,128)S(1)}, f32[6,256]{1,0:T(8,128)S(1)}) custom-call(s32[1,6]{1,0:T(1,128)S(1)} %bitcast.34, f32[576,256]{1,0:T(8,128)S(1)} %get-tuple-element.38.refs_1_, f32[576,576]{1,0:T(8,128)S(1)} %bitcast.25, f32[48,576]{1,0:T(8,128)S(1)} %bitcast.20, f32[576,256]{1,0:T(8,128)S(1)} %get-tuple-element.39.refs_1_.refs_4_.refs_2_, ...), custom_call_target="tpu_custom_call" | custom-call | flops 1189085184 | bytes 5081088 | tf_op jit(solution)/shard_map/pallas_call | solution.py:63
  187.9 0.1 all_to_all.22
  188.0 21.2 %all_to_all.33 = f32[32,1,48]{2,1,0:T(1,128)S(1)} all-to-all(f32[32,1,48]{2,1,0:T(1,128)S(1)} %bitcast.38), channel_id=1, replica_groups=mesh['y'=4,'z'=32,'core'=2,'grp'=4] {'y','core','grp'}, dimensions={0} | all-to-all | bytes 12288 | tf_op jit(solution)/shard_map/all_to_all | solution.py:36
  209.2 0.1 reduce_sum.18
  209.3 36.6 %all_to_all.34 = f32[32,1,48]{2,1,0:T(1,128)S(1)} all-to-all(f32[32,1,48]{2,1,0:T(1,128)S(1)} %broadcast_in_dim.6), channel_id=1, replica_groups=mesh['y'=4,'z'=32,'core'=2,'grp'=4] {'z'}, dimensions={0} | all-to-all | bytes 12288 | tf_op jit(solution)/shard_map/all_to_all | solution.py:36
  246.0 12.0 %all_to_all.35 = f32[32,1,48]{2,1,0:T(1,128)S(1)} all-to-all(f32[32,1,48]{2,1,0:T(1,128)S(1)} %broadcast_in_dim.7), channel_id=1, replica_groups=mesh['y'=4,'z'=32,'core'=2,'grp'=4] {'y','core','grp'}, dimensions={0} | all-to-all | bytes 12288 | tf_op jit(solution)/shard_map/all_to_all | solution.py:36
  258.0 0.5 broadcast.9
  258.5 0.7 reduce.5
  259.2 0.1 reshape.34.refs_1_
  259.3 1.7 shard_map.85
  (14 shorter events, 0.1 us)
Async XLA Ops:
  0.6 109.8 %copy-start.7 = (s32[1,1,6]{2,1,0:T(1,128)S(1)}, s32[1,1,6]{2,1,0:T(1,128)}, u32[]{:S(2)}) copy-start(s32[1,1,6]{2,1,0:T(1,128)} %param.11) | copy-start | bytes 76
  0.6 1.1 copy-start
  1.7 0.9 copy-start.1
  2.6 0.8 copy-start.4
  3.4 74.9 %copy-start.5 = (f32[1,1,48,192]{3,2,1,0:T(8,128)S(1)}, f32[1,1,48,192]{3,2,1,0:T(8,128)}, u32[]{:S(2)}) copy-start(f32[1,1,48,192]{3,2,1,0:T(8,128)} %param.9) | copy-start | bytes 110596
  3.4 107.0 %copy-start.2 = (f32[1,1,576,48]{2,3,1,0:T(8,128)S(1)}, f32[1,1,576,48]{2,3,1,0:T(8,128)}, u32[]{:S(2)}) copy-start(f32[1,1,576,48]{2,3,1,0:T(8,128)} %param.8) | copy-start | bytes 331780
  3.4 107.0 %copy-start.3 = (f32[1,1,576,576]{3,2,1,0:T(8,128)S(1)}, f32[1,1,576,576]{3,2,1,0:T(8,128)}, u32[]{:S(2)}) copy-start(f32[1,1,576,576]{3,2,1,0:T(8,128)} %param.6) | copy-start | bytes 3981316
  3.5 26.9 %collective-permute-start = (f32[120,256]{1,0:T(8,128)S(1)}, f32[120,256]{1,0:T(8,128)S(1)}, u32[]{:S(2)}, u32[]{:S(2)}) collective-permute-start(f32[120,256]{1,0:T(8,128)S(1)} %get-tuple-element.24), channel_id=1, source_target_pairs={{0,4},{4,8},{8,12},{12,16},{16,20},{20,24},{24,28},{28,32},{32,36}... | collective-permute-start | bytes 368648 | tf_op jit(solution)/shard_map/ppermute | solution.py:24
  8.6 58.1 %collective-permute-start.4 = (f32[168,256]{1,0:T(8,128)S(1)}, f32[168,256]{1,0:T(8,128)S(1)}, u32[]{:S(2)}, u32[]{:S(2)}) collective-permute-start(f32[168,256]{1,0:T(8,128)S(1)} %get-tuple-element.28), channel_id=1, source_target_pairs={{0,1},{1,2},{2,3},{4,5},{5,6},{6,7},{8,9},{9,10},{10,11},{12,13},{... | collective-permute-start | bytes 516104 | tf_op jit(solution)/shard_map/ppermute | solution.py:24
  11.7 55.0 %collective-permute-start.5 = (f32[168,256]{1,0:T(8,128)S(1)}, f32[168,256]{1,0:T(8,128)S(1)}, u32[]{:S(2)}, u32[]{:S(2)}) collective-permute-start(f32[168,256]{1,0:T(8,128)S(1)} %get-tuple-element.29), channel_id=1, source_target_pairs={{1,0},{2,1},{3,2},{5,4},{6,5},{7,6},{9,8},{10,9},{11,10},{13,12},{... | collective-permute-start | bytes 516104 | tf_op jit(solution)/shard_map/ppermute | solution.py:24
  13.0 18.7 %collective-permute-start.1 = (f32[120,256]{1,0:T(8,128)S(1)}, f32[120,256]{1,0:T(8,128)S(1)}, u32[]{:S(2)}, u32[]{:S(2)}) collective-permute-start(f32[120,256]{1,0:T(8,128)S(1)} %get-tuple-element.25), channel_id=1, source_target_pairs={{4,0},{8,4},{12,8},{16,12},{20,16},{24,20},{28,24},{32,28},{36,32}... | collective-permute-start | bytes 368648 | tf_op jit(solution)/shard_map/ppermute | solution.py:24
  23.6 8.7 %collective-permute-start.2 = (f32[120,256]{1,0:T(8,128)S(1)}, f32[120,256]{1,0:T(8,128)S(1)}, u32[]{:S(2)}, u32[]{:S(2)}) collective-permute-start(f32[120,256]{1,0:T(8,128)S(1)} %get-tuple-element.26), channel_id=1, source_target_pairs={{0,64},{4,68},{8,72},{12,76},{16,80},{20,84},{24,88},{28,92},{32,9... | collective-permute-start | bytes 368648 | tf_op jit(solution)/shard_map/ppermute | solution.py:24
  30.4 36.3 %collective-permute-start.3 = (f32[120,256]{1,0:T(8,128)S(1)}, f32[120,256]{1,0:T(8,128)S(1)}, u32[]{:S(2)}, u32[]{:S(2)}) collective-permute-start(f32[120,256]{1,0:T(8,128)S(1)} %get-tuple-element.27), channel_id=1, source_target_pairs={{64,0},{68,4},{72,8},{76,12},{80,16},{84,20},{88,24},{92,28},{96,3... | collective-permute-start | bytes 368648 | tf_op jit(solution)/shard_map/ppermute | solution.py:24
  66.7 0.7 copy-start.6
  78.5 19.6 %collective-permute-start.6 = (f32[48,256]{1,0:T(8,128)S(1)}, f32[48,256]{1,0:T(8,128)S(1)}, u32[]{:S(2)}, u32[]{:S(2)}) collective-permute-start(f32[48,256]{1,0:T(8,128)S(1)} %shard_map.79.refs_5_), channel_id=1, source_target_pairs={{0,4},{4,8},{8,12},{12,16},{16,20},{20,24},{24,28},{28,32},{32,36}... | collective-permute-start | bytes 147464 | tf_op jit(solution)/shard_map/ppermute | solution.py:24
  81.9 16.3 %collective-permute-start.7 = (f32[48,256]{1,0:T(8,128)S(1)}, f32[48,256]{1,0:T(8,128)S(1)}, u32[]{:S(2)}, u32[]{:S(2)}) collective-permute-start(f32[48,256]{1,0:T(8,128)S(1)} %shard_map.79.refs_5_), channel_id=1, source_target_pairs={{4,0},{8,4},{12,8},{16,12},{20,16},{24,20},{28,24},{32,28},{36,32}... | collective-permute-start | bytes 147464 | tf_op jit(solution)/shard_map/ppermute | solution.py:24
  84.1 14.0 %collective-permute-start.8 = (f32[48,256]{1,0:T(8,128)S(1)}, f32[48,256]{1,0:T(8,128)S(1)}, u32[]{:S(2)}, u32[]{:S(2)}) collective-permute-start(f32[48,256]{1,0:T(8,128)S(1)} %shard_map.79.refs_5_), channel_id=1, source_target_pairs={{0,64},{4,68},{8,72},{12,76},{16,80},{20,84},{24,88},{28,92},{32,9... | collective-permute-start | bytes 147464 | tf_op jit(solution)/shard_map/ppermute | solution.py:24
  96.8 13.6 %collective-permute-start.9 = (f32[48,256]{1,0:T(8,128)S(1)}, f32[48,256]{1,0:T(8,128)S(1)}, u32[]{:S(2)}, u32[]{:S(2)}) collective-permute-start(f32[48,256]{1,0:T(8,128)S(1)} %shard_map.79.refs_5_), channel_id=1, source_target_pairs={{64,0},{68,4},{72,8},{76,12},{80,16},{84,20},{88,24},{92,28},{96,3... | collective-permute-start | bytes 147464 | tf_op jit(solution)/shard_map/ppermute | solution.py:24
  114.9 17.9 %collective-permute-start.10 = (f32[96,256]{1,0:T(8,128)S(1)}, f32[96,256]{1,0:T(8,128)S(1)}, u32[]{:S(2)}, u32[]{:S(2)}) collective-permute-start(f32[96,256]{1,0:T(8,128)S(1)} %get-tuple-element.33.refs_3_), channel_id=1, source_target_pairs={{0,4},{4,8},{8,12},{12,16},{16,20},{20,24},{24,28},{28,32},{32,36}... | collective-permute-start | bytes 294920 | tf_op jit(solution)/shard_map/ppermute | solution.py:24
  118.4 15.6 %collective-permute-start.11 = (f32[96,256]{1,0:T(8,128)S(1)}, f32[96,256]{1,0:T(8,128)S(1)}, u32[]{:S(2)}, u32[]{:S(2)}) collective-permute-start(f32[96,256]{1,0:T(8,128)S(1)} %get-tuple-element.32.refs_2_), channel_id=1, source_target_pairs={{4,0},{8,4},{12,8},{16,12},{20,16},{24,20},{28,24},{32,28},{36,32}... | collective-permute-start | bytes 294920 | tf_op jit(solution)/shard_map/ppermute | solution.py:24
  122.4 14.8 %collective-permute-start.12 = (f32[96,256]{1,0:T(8,128)S(1)}, f32[96,256]{1,0:T(8,128)S(1)}, u32[]{:S(2)}, u32[]{:S(2)}) collective-permute-start(f32[96,256]{1,0:T(8,128)S(1)} %get-tuple-element.35.refs_5_), channel_id=1, source_target_pairs={{0,64},{4,68},{8,72},{12,76},{16,80},{20,84},{24,88},{28,92},{32,9... | collective-permute-start | bytes 294920 | tf_op jit(solution)/shard_map/ppermute | solution.py:24
  129.2 17.3 %collective-permute-start.13 = (f32[96,256]{1,0:T(8,128)S(1)}, f32[96,256]{1,0:T(8,128)S(1)}, u32[]{:S(2)}, u32[]{:S(2)}) collective-permute-start(f32[96,256]{1,0:T(8,128)S(1)} %get-tuple-element.34.refs_4_), channel_id=1, source_target_pairs={{64,0},{68,4},{72,8},{76,12},{80,16},{84,20},{88,24},{92,28},{96,3... | collective-permute-start | bytes 294920 | tf_op jit(solution)/shard_map/ppermute | solution.py:24
  130.5 16.0 %collective-permute-start.14 = (f32[96,256]{1,0:T(8,128)S(1)}, f32[96,256]{1,0:T(8,128)S(1)}, u32[]{:S(2)}, u32[]{:S(2)}) collective-permute-start(f32[96,256]{1,0:T(8,128)S(1)} %get-tuple-element.37.refs_7_), channel_id=1, source_target_pairs={{0,1},{1,2},{2,3},{4,5},{5,6},{6,7},{8,9},{9,10},{10,11},{12,13},{... | collective-permute-start | bytes 294920 | tf_op jit(solution)/shard_map/ppermute | solution.py:24
  132.7 13.8 %collective-permute-start.15 = (f32[96,256]{1,0:T(8,128)S(1)}, f32[96,256]{1,0:T(8,128)S(1)}, u32[]{:S(2)}, u32[]{:S(2)}) collective-permute-start(f32[96,256]{1,0:T(8,128)S(1)} %get-tuple-element.36.refs_6_), channel_id=1, source_target_pairs={{1,0},{2,1},{3,2},{5,4},{6,5},{7,6},{9,8},{10,9},{11,10},{13,12},{... | collective-permute-start | bytes 294920 | tf_op jit(solution)/shard_map/ppermute | solution.py:24
  155.3 18.1 %collective-permute-start.16 = (f32[48,256]{1,0:T(8,128)S(1)}, f32[48,256]{1,0:T(8,128)S(1)}, u32[]{:S(2)}, u32[]{:S(2)}) collective-permute-start(f32[48,256]{1,0:T(8,128)S(1)} %shard_map.83.refs_6_), channel_id=1, source_target_pairs={{0,4},{4,8},{8,12},{12,16},{16,20},{20,24},{24,28},{28,32},{32,36}... | collective-permute-start | bytes 147464 | tf_op jit(solution)/shard_map/ppermute | solution.py:24
  158.0 15.4 %collective-permute-start.17 = (f32[48,256]{1,0:T(8,128)S(1)}, f32[48,256]{1,0:T(8,128)S(1)}, u32[]{:S(2)}, u32[]{:S(2)}) collective-permute-start(f32[48,256]{1,0:T(8,128)S(1)} %shard_map.83.refs_6_), channel_id=1, source_target_pairs={{4,0},{8,4},{12,8},{16,12},{20,16},{24,20},{28,24},{32,28},{36,32}... | collective-permute-start | bytes 147464 | tf_op jit(solution)/shard_map/ppermute | solution.py:24
  161.0 12.4 %collective-permute-start.18 = (f32[48,256]{1,0:T(8,128)S(1)}, f32[48,256]{1,0:T(8,128)S(1)}, u32[]{:S(2)}, u32[]{:S(2)}) collective-permute-start(f32[48,256]{1,0:T(8,128)S(1)} %shard_map.83.refs_6_), channel_id=1, source_target_pairs={{0,64},{4,68},{8,72},{12,76},{16,80},{20,84},{24,88},{28,92},{32,9... | collective-permute-start | bytes 147464 | tf_op jit(solution)/shard_map/ppermute | solution.py:24
  170.5 13.5 %collective-permute-start.19 = (f32[48,256]{1,0:T(8,128)S(1)}, f32[48,256]{1,0:T(8,128)S(1)}, u32[]{:S(2)}, u32[]{:S(2)}) collective-permute-start(f32[48,256]{1,0:T(8,128)S(1)} %shard_map.83.refs_6_), channel_id=1, source_target_pairs={{64,0},{68,4},{72,8},{76,12},{80,16},{84,20},{88,24},{92,28},{96,3... | collective-permute-start | bytes 147464 | tf_op jit(solution)/shard_map/ppermute | solution.py:24

commit v4 on v3

v4 whole, which is shorter than its diff:
```python
import functools
import math

import jax
import jax.numpy as jnp
from jax import lax
from jax.experimental import pallas as pl
from jax.experimental.pallas import tpu as pltpu
from jax.sharding import Mesh, PartitionSpec as P


SUBROW = 16
SLOTS = 6
LANES = 128
PLANE = ("y", "core", "grp")
SUB = ("y", "z", "core")
SOURCES = ((SUB, -1), (SUB, 1), (SUB, -SUBROW), (SUB, SUBROW), ("grp", -1), ("grp", 1))
ORDER = (2, 3, 0, 1, 4, 5)


def fetch(piece, slot):
    axis, offset = SOURCES[slot]
    count = lax.axis_size(axis)
    pairs = [(i, i - offset) for i in range(count) if 0 <= i - offset < count]
    return lax.ppermute(piece, axis, pairs)


def exchange(pieces):
    gotten = [None] * len(pieces)
    for slot in ORDER:
        if slot < len(pieces):
            gotten[slot] = fetch(pieces[slot], slot)
    return gotten


def swap(blocks, axes):
    return lax.all_to_all(blocks, axes, 0, 0, tiled=True)


def total(terms):
    plane = lax.axis_size(PLANE)
    chunks = terms.reshape(plane, -1)
    chunk = jnp.sum(swap(chunks, PLANE), axis=0)
    chunk = jnp.sum(swap(jnp.broadcast_to(chunk, (lax.axis_size("z"),) + chunk.shape), "z"), axis=0)
    return swap(jnp.broadcast_to(chunk, chunks.shape), PLANE).reshape(terms.shape)


def dot(left, right, across=1):
    return lax.dot_general(
        left, right, (((across,), (0,)), ((), ())),
        precision=lax.Precision.HIGHEST, preferred_element_type=jnp.float32,
    )


def clamp(values, slot, touching):
    bounded = jnp.maximum(values, 0.0) if slot % 2 else jnp.minimum(values, 0.0)
    return jnp.where(touching, bounded, values)


def kernel_call(body, flags, arrays, outs, flops):
    smem = pl.BlockSpec(memory_space=pltpu.SMEM)
    vmem = pl.BlockSpec(memory_space=pltpu.VMEM)
    moved = sum(a.size for a in arrays) + sum(math.prod(o) for o in outs)
    return pl.pallas_call(
        functools.partial(body, len(flags), len(arrays)),
        out_shape=[jax.ShapeDtypeStruct(o, jnp.float32) for o in outs],
        in_specs=[smem] * len(flags) + [vmem] * len(arrays),
        out_specs=[vmem] * len(outs),
        compiler_params=pltpu.CompilerParams(vmem_limit_bytes=24 << 20),
        cost_estimate=pl.CostEstimate(flops=flops, bytes_accessed=4 * moved, transcendentals=0),
    )(*flags, *arrays)


def split(refs, flags, arrays):
    return refs[:flags], refs[flags:flags + arrays], refs[flags + arrays:]


def pack_kernel(gap, shapes, rows, *refs):
    outs, (shapes_here, rows_here, sems) = refs[:SLOTS], refs[SLOTS:]
    face = gap.shape[0] // SLOTS
    half = shapes.shape[0] // 2
    copies = [
        pltpu.make_async_copy(shapes, shapes_here, sems.at[0]),
        pltpu.make_async_copy(rows, rows_here, sems.at[1]),
    ]
    for slot, out in enumerate(outs):
        piece = gap.at[pl.ds((slot ^ 1) * face, face)]
        copies.append(pltpu.make_async_copy(piece, out.at[pl.ds(0, face)], sems.at[2 + slot]))
    for copy in copies:
        copy.start()
    copies[0].wait()
    for slot, out in enumerate(outs):
        piece = shapes_here[:, (slot ^ 1) * face:(slot ^ 1) * face + face]
        out[face:face + half] = jnp.zeros((half, out.shape[1]), jnp.float32)
        out[face:face + half, :face] = piece[:half]
        out[face:face + half, LANES:LANES + face] = piece[half:]
    copies[1].wait()
    for out in outs[4:]:
        out[face + half:] = jnp.zeros((2 * half, out.shape[1]), jnp.float32)
        out[face + half:, :rows.shape[1]] = rows_here[...]
    for copy in copies[2:]:
        copy.wait()


def pack(gap, shapes, rows):
    face = gap.shape[0] // SLOTS
    short = face + shapes.shape[0] // 2
    heights = [short] * 4 + [short + shapes.shape[0]] * 2
    hbm = pl.BlockSpec(memory_space=pltpu.HBM)
    vmem = pl.BlockSpec(memory_space=pltpu.VMEM)
    return pl.pallas_call(
        pack_kernel,
        out_shape=[jax.ShapeDtypeStruct((height, gap.shape[1]), jnp.float32) for height in heights],
        in_specs=[hbm] * 3,
        out_specs=[vmem] * SLOTS,
        scratch_shapes=[
            pltpu.VMEM(shapes.shape, jnp.float32), pltpu.VMEM(rows.shape, jnp.float32),
            pltpu.SemaphoreType.DMA((2 + SLOTS,)),
        ],
        compiler_params=pltpu.CompilerParams(vmem_limit_bytes=67043328),
        name="pack",
    )(gap, shapes, rows)


def flags_kernel(nf, na, *refs):
    (live, contact), (gap, shapes), (flags, masked, kept) = split(refs, nf, na)
    face = gap.shape[0] // SLOTS
    for slot in range(SLOTS):
        shape = (1, flags.shape[1])
        rows = slice(slot * face, (slot + 1) * face)
        flags[slot:slot + 1] = jnp.full(shape, live[0, slot], jnp.int32).astype(jnp.float32)
        flags[8 + slot:9 + slot] = jnp.full(shape, contact[0, slot], jnp.int32).astype(jnp.float32)
        masked[rows] = flags[slot:slot + 1] * gap[rows]
    kept[...] = shapes[...]


def residual_kernel(nf, na, *refs):
    _, (flags, masked, shapes, *gotten), (values, spread) = split(refs, nf, na)
    face = values.shape[0] // SLOTS
    for slot in range(SLOTS):
        rows = slice(slot * face, (slot + 1) * face)
        values[rows] = flags[slot:slot + 1] * gotten[slot][:face] - masked[rows]
    coef = dot(shapes[...], values[...])
    for row in range(spread.shape[0]):
        spread[row] = coef


def opened_kernel(nf, na, *refs):
    _, (flags, shapes, *faces), (values, spread) = split(refs, nf, na)
    pushed, gotten = faces[:SLOTS], faces[SLOTS:]
    face = values.shape[0] // SLOTS
    for slot in range(SLOTS):
        rows = slice(slot * face, (slot + 1) * face)
        values[rows] = flags[slot:slot + 1] * (pushed[slot][...] - gotten[slot][...])
    coef = dot(shapes[...], values[...])
    for row in range(spread.shape[0]):
        spread[row] = coef


def coarse_kernel(nf, na, *refs):
    _, (rows, coefs), (own,) = split(refs, nf, na)
    own[...] = dot(rows[...], coefs[...])


def pairs_kernel(nf, na, *refs):
    (live,), (shapes, *messages), (pairs,) = split(refs, nf, na)
    face = pairs.shape[0] // SLOTS
    half = shapes.shape[0] // 2
    for slot in range(SLOTS):
        rows = slice(slot * face, (slot + 1) * face)
        packed = messages[slot][face:face + half]
        both = jnp.concatenate([shapes[:, rows], -packed[:, :face], -packed[:, LANES:LANES + face]])
        pairs[rows] = live[0, slot].astype(jnp.float32) * both.T


def beside_kernel(nf, na, *refs):
    _, (coefs, *messages), outs = split(refs, nf, na)
    for message, out in zip(messages, outs):
        out[...] = dot(message[message.shape[0] - out.shape[0]:, :coefs.shape[0]], coefs[...])


def corrected(values, pairs, own, near):
    face = values.shape[0] // SLOTS
    faces = []
    for slot in range(SLOTS):
        rows = slice(slot * face, (slot + 1) * face)
        faces.append(values[rows] - dot(pairs[rows], jnp.concatenate([own[...], near[slot][...]])))
    return faces


def push_kernel(nf, na, *refs):
    _, (flags, values, operator, pairs, own, *near), (first, push, *far) = split(refs, nf, na)
    face = values.shape[0] // SLOTS
    for slot, part in enumerate(corrected(values, pairs, own, near)):
        rows = slice(slot * face, (slot + 1) * face)
        first[rows] = part
        push[rows] = clamp(-part, slot, flags[8 + slot:9 + slot] > 0.0)
    image = dot(operator[2 * face:4 * face], push[...])
    for at, out in enumerate(far):
        out[...] = image[at * face:(at + 1) * face]


def rest_kernel(nf, na, *refs):
    _, (operator, push), outs = split(refs, nf, na)
    face = operator.shape[0] // SLOTS
    upper = dot(operator[:2 * face], push[...])
    lower = dot(operator[4 * face:], push[...])
    outs[0][...] = upper[:face]
    outs[1][...] = upper[face:]
    outs[2][...] = lower[:face]
    outs[3][...] = lower[face:]


def inner(left, right):
    return jnp.sum(left * right, axis=0, keepdims=True)


def image_kernel(nf, na, *refs):
    _, (operator, first), (image, sums) = split(refs, nf, na)
    image[...] = dot(operator[...], first[...])
    sums[0:1] = inner(first[...], first[...])
    sums[1:2] = inner(first[...], image[...])


def change_kernel(nf, na, *refs):
    _, (values, operator, pairs, first, image, early, own, *near), (change, sums) = split(refs, nf, na)
    face = values.shape[0] // SLOTS
    for slot, part in enumerate(corrected(values, pairs, own, near)):
        change[slot * face:(slot + 1) * face] = part
    moved = dot(operator[...], change[...])
    sums[0:2] = early[...]
    sums[2:3] = inner(first[...], change[...])
    sums[3:4] = inner(change[...], change[...])
    sums[4:5] = inner(change[...], image[...])
    sums[5:6] = inner(change[...], moved)


def finish_kernel(nf, na, *refs):
    _, (flags, sums, first, push, change), (multipliers, direction) = split(refs, nf, na)
    face = first.shape[0] // SLOTS
    s = [sums[i:i + 1] for i in range(6)]
    step = s[0] / (2.0 * s[1])
    norm = s[0] + step * (2.0 * s[2] + step * s[3])
    curvature = 2.0 * (s[1] + step * (2.0 * s[4] + step * s[5]))
    ratio = norm / curvature
    for slot in range(SLOTS):
        rows = slice(slot * face, (slot + 1) * face)
        part = first[rows] + step * change[rows]
        direction[rows] = part
        multipliers[rows] = clamp(step * push[rows] - ratio * part, slot, flags[8 + slot:9 + slot] > 0.0)


def body(dual_ops, gap_parts, modes, coarse_rows, face_live, contact):
    operator = dual_ops[0, 0]
    dual_rows = operator.shape[0]
    face = dual_rows // SLOTS
    cases = gap_parts.shape[3]
    kinds = modes.shape[3]
    groups = lax.axis_size("grp")
    live, touching = face_live[0], contact[0]
    rows = coarse_rows[0, 0]
    parts = gap_parts[0, 0]
    shapes = modes[0, 0].T
    whole = (dual_rows, cases)
    spread = (groups, kinds, cases)
    heavy = 12 * dual_rows * dual_rows * cases
    light = 12 * dual_rows * kinds * cases

    messages = exchange(pack(parts, shapes, rows))
    flags, masked, shapes = kernel_call(
        flags_kernel, [live, touching], [parts, shapes], [(16, cases), whole, shapes.shape], 0
    )

    def coarse(spread_coef):
        coefs = swap(spread_coef, "grp").reshape(groups * kinds, cases)
        own, = kernel_call(coarse_kernel, [], [rows, coefs], [(kinds, cases)], light // 3)
        near = exchange([own] * 4)
        beside = kernel_call(beside_kernel, [], [coefs, *messages[4:]], [(kinds, cases)] * 2, light)
        return [own, *near, *beside]

    values, coef = kernel_call(residual_kernel, [], [flags, masked, shapes, *messages], [whole, spread], light)
    known = coarse(coef)
    pairs, = kernel_call(pairs_kernel, [live], [shapes, *messages], [(dual_rows, 2 * kinds)], light)
    first, push, *far = kernel_call(
        push_kernel, [], [flags, values, operator, pairs, *known], [whole, whole] + [(face, cases)] * 2,
        heavy // 3 + 2 * light,
    )
    rest = kernel_call(rest_kernel, [], [operator, push], [(face, cases)] * 4, 2 * heavy // 3)
    pushed = [*rest[:2], *far, *rest[2:]]
    gotten = exchange([pushed[slot ^ 1] for slot in range(SLOTS)])
    image, early = kernel_call(image_kernel, [], [operator, first], [whole, (2, cases)], heavy)
    values, coef = kernel_call(opened_kernel, [], [flags, shapes, *pushed, *gotten], [whole, spread], light)
    known = coarse(coef)
    change, sums = kernel_call(
        change_kernel, [], [values, operator, pairs, first, image, early, *known],
        [whole, (6, cases)], heavy + 2 * light,
    )
    multipliers, direction = kernel_call(
        finish_kernel, [], [flags, total(sums), first, push, change], [whole, whole], 8 * dual_rows * cases
    )
    shape = (1, 1) + whole
    return (multipliers.reshape(shape), direction.reshape(shape))


def solution(mesh):
    fine = Mesh(mesh.devices.reshape(4, 32, 2, 4), ("y", "z", "core", "grp"))
    wide = P(SUB, "grp", None, None)
    flags = P(SUB, "grp", None)
    return jax.shard_map(
        body, mesh=fine, in_specs=(wide, wide, wide, wide, flags, flags), out_specs=(wide, wide), check_vma=False
    )
```

time: 262 us -> 261 us (level)
  blocking collectives: 87.3 us -> 90.3 us
    pallas_call x9 -> x13, Pallas kernels: 14.2 us -> 11.1 us  [kernel_call(): pl.pallas_call(functools.partial(body, len(flags), len(arrays)), out_shap...]
    all_to_all x5, blocking collectives: 87.3 us -> 90.3 us  [swap(): return lax.all_to_all(blocks, axes, 0, 0, tiled=True)]
  transfers between devices with their start and end apart: 20 -> 20, of which waited for: 6 -> 5; matrix products, arithmetic and copies ran while one was open for 0% -> 0% of each run, Pallas kernels for 1% -> 1%
where the time goes in v4:
time: 261 us; the launch traced here: 260 us
  blocking collectives  90.3 us (35%)
  starting transfers between devices  82.7 us (32%)
  waiting for transfers between devices  67.8 us (26%)
  Pallas kernels  13.2 us (5%)
  local copies, waits for them, and re-layouts  3.97 us (2%)
    all_to_all x5, blocking collectives, swap(): return lax.all_to_all(blocks, axes, 0, 0, tiled=True)  90.3 us
    ppermute x20, starting transfers between devices, fetch(): return lax.ppermute(piece, axis, pairs)  82.7 us
    ppermute x20, waiting for transfers between devices, fetch(): return lax.ppermute(piece, axis, pairs)  67.8 us
    pallas_call x13, Pallas kernels, kernel_call(): pl.pallas_call(functools.partial(body, len(flags), len(arrays)), out_shap...  11.1 us
  transfers between devices with their start and end apart: 20, of which 5 were waited for; matrix products, arithmetic and copies ran while one was open for 0% of the time, Pallas kernels for 1%

profile of v4, /device:TPU:1, one launch (start us, length us, event | category | flops | bytes accessed | tf_op | source)
XLA Modules:
  0.0 259.8 jit_solution(9119886074148544254)
XLA Ops:
  0.6 2.2 pack.1
  2.8 4.9 %collective-permute-start = (f32[120,256]{1,0:T(8,128)}, f32[120,256]{1,0:T(8,128)S(1)}, u32[]{:S(2)}, u32[]{:S(2)}) collective-permute-start(f32[120,256]{1,0:T(8,128)} %get-tuple-element.36), channel_id=1, source_target_pairs={{0,4},{4,8},{8,12},{12,16},{16,20},{20,24},{24,28},{28,32},{32,36}... | collective-permute-start | bytes 368648 | tf_op jit(solution)/shard_map/ppermute | solution.py:25
  7.7 3.1 %collective-permute-start.4 = (f32[168,256]{1,0:T(8,128)}, f32[168,256]{1,0:T(8,128)S(1)}, u32[]{:S(2)}, u32[]{:S(2)}) collective-permute-start(f32[168,256]{1,0:T(8,128)} %get-tuple-element.40), channel_id=1, source_target_pairs={{0,1},{1,2},{2,3},{4,5},{5,6},{6,7},{8,9},{9,10},{10,11},{12,13},{... | collective-permute-start | bytes 516104 | tf_op jit(solution)/shard_map/ppermute | solution.py:25
  10.9 1.3 collective-permute-start.5
  12.2 10.6 %collective-permute-start.1 = (f32[120,256]{1,0:T(8,128)}, f32[120,256]{1,0:T(8,128)S(1)}, u32[]{:S(2)}, u32[]{:S(2)}) collective-permute-start(f32[120,256]{1,0:T(8,128)} %get-tuple-element.37), channel_id=1, source_target_pairs={{4,0},{8,4},{12,8},{16,12},{20,16},{24,20},{28,24},{32,28},{36,32}... | collective-permute-start | bytes 368648 | tf_op jit(solution)/shard_map/ppermute | solution.py:25
  22.7 6.8 %collective-permute-start.2 = (f32[120,256]{1,0:T(8,128)}, f32[120,256]{1,0:T(8,128)S(1)}, u32[]{:S(2)}, u32[]{:S(2)}) collective-permute-start(f32[120,256]{1,0:T(8,128)} %get-tuple-element.38), channel_id=1, source_target_pairs={{0,64},{4,68},{8,72},{12,76},{16,80},{20,84},{24,88},{28,92},{32,9... | collective-permute-start | bytes 368648 | tf_op jit(solution)/shard_map/ppermute | solution.py:25
  29.5 0.0 collective-permute-done.refs_3_.refs_2_
  29.6 1.3 collective-permute-start.3
  30.9 0.0 copy-start
  30.9 1.1 copy-done
  31.9 0.9 copy-done.2
  32.8 0.7 copy-done.4
  33.5 0.7 copy-done.5
  34.1 0.6 shard_map.77
  34.7 0.0 collective-permute-done.1.refs_4_.refs_3_
  34.8 0.0 collective-permute-done.2.refs_5_.refs_4_
  34.8 31.3 %collective-permute-done.3.refs_6_.refs_5_ = f32[120,256]{1,0:T(8,128)S(1)} collective-permute-done((f32[120,256]{1,0:T(8,128)}, f32[120,256]{1,0:T(8,128)S(1)}, u32[]{:S(2)}, u32[]{:S(2)}) %collective-permute-start.3) | collective-permute-done | bytes 122912 | tf_op jit(solution)/shard_map/ppermute | solution.py:25
  66.1 0.5 shard_map.78
  66.6 0.0 copy-start.1
  66.6 10.0 %all_to_all.31 = f32[4,48,256]{2,1,0:T(8,128)S(1)} all-to-all(f32[4,48,256]{2,1,0:T(8,128)S(1)} %get-tuple-element.43), channel_id=1, replica_groups=mesh['y'=4,'z'=32,'core'=2,'grp'=4] {'grp'}, dimensions={0} | all-to-all | bytes 393216 | tf_op jit(solution)/shard_map/all_to_all | solution.py:37
  76.6 0.2 shard_map.80.refs_4_
  76.8 3.3 %collective-permute-start.6 = (f32[48,256]{1,0:T(8,128)S(1)}, f32[48,256]{1,0:T(8,128)S(1)}, u32[]{:S(2)}, u32[]{:S(2)}) collective-permute-start(f32[48,256]{1,0:T(8,128)S(1)} %shard_map.80.refs_4_), channel_id=1, source_target_pairs={{0,4},{4,8},{8,12},{12,16},{16,20},{20,24},{24,28},{28,32},{32,36}... | collective-permute-start | bytes 147464 | tf_op jit(solution)/shard_map/ppermute | solution.py:25
  80.1 2.2 collective-permute-start.7
  82.4 12.7 %collective-permute-start.8 = (f32[48,256]{1,0:T(8,128)S(1)}, f32[48,256]{1,0:T(8,128)S(1)}, u32[]{:S(2)}, u32[]{:S(2)}) collective-permute-start(f32[48,256]{1,0:T(8,128)S(1)} %shard_map.80.refs_4_), channel_id=1, source_target_pairs={{0,64},{4,68},{8,72},{12,76},{16,80},{20,84},{24,88},{28,92},{32,9... | collective-permute-start | bytes 147464 | tf_op jit(solution)/shard_map/ppermute | solution.py:25
  95.1 1.3 collective-permute-start.9
  96.4 0.9 shard_map.79.refs_3_.refs_2_
  97.3 0.3 shard_map.81
  97.6 0.0 collective-permute-done.6.refs_5_
  97.6 0.0 collective-permute-done.7.refs_6_
  97.7 11.1 %collective-permute-done.9.refs_8_ = f32[48,256]{1,0:T(8,128)S(1)} collective-permute-done((f32[48,256]{1,0:T(8,128)S(1)}, f32[48,256]{1,0:T(8,128)S(1)}, u32[]{:S(2)}, u32[]{:S(2)}) %collective-permute-start.9) | collective-permute-done | bytes 49184 | tf_op jit(solution)/shard_map/ppermute | solution.py:25
  108.7 1.3 shard_map.82
  110.0 1.2 shard_map.83
  111.2 3.5 %collective-permute-start.10 = (f32[96,256]{1,0:T(8,128)S(1)}, f32[96,256]{1,0:T(8,128)S(1)}, u32[]{:S(2)}, u32[]{:S(2)}) collective-permute-start(f32[96,256]{1,0:T(8,128)S(1)} %get-tuple-element.48.refs_3_), channel_id=1, source_target_pairs={{0,4},{4,8},{8,12},{12,16},{16,20},{20,24},{24,28},{28,32},{32,36}... | collective-permute-start | bytes 294920 | tf_op jit(solution)/shard_map/ppermute | solution.py:25
  114.8 4.0 %collective-permute-start.11 = (f32[96,256]{1,0:T(8,128)S(1)}, f32[96,256]{1,0:T(8,128)S(1)}, u32[]{:S(2)}, u32[]{:S(2)}) collective-permute-start(f32[96,256]{1,0:T(8,128)S(1)} %get-tuple-element.47.refs_2_), channel_id=1, source_target_pairs={{4,0},{8,4},{12,8},{16,12},{20,16},{24,20},{28,24},{32,28},{36,32}... | collective-permute-start | bytes 294920 | tf_op jit(solution)/shard_map/ppermute | solution.py:25
  118.8 2.2 collective-permute-start.14
  121.0 1.3 collective-permute-start.15
  122.3 6.9 %collective-permute-start.12 = (f32[96,256]{1,0:T(8,128)S(1)}, f32[96,256]{1,0:T(8,128)S(1)}, u32[]{:S(2)}, u32[]{:S(2)}) collective-permute-start(f32[96,256]{1,0:T(8,128)S(1)} %get-tuple-element.50.refs_5_), channel_id=1, source_target_pairs={{0,64},{4,68},{8,72},{12,76},{16,80},{20,84},{24,88},{28,92},{32,9... | collective-permute-start | bytes 294920 | tf_op jit(solution)/shard_map/ppermute | solution.py:25
  129.2 0.0 collective-permute-done.10.refs_8_
  129.2 1.3 collective-permute-start.13
  130.5 0.0 collective-permute-done.14.refs_12_
  130.5 0.0 collective-permute-done.15.refs_13_
  130.5 7.0 %collective-permute-done.12.refs_10_ = f32[96,256]{1,0:T(8,128)S(1)} collective-permute-done((f32[96,256]{1,0:T(8,128)S(1)}, f32[96,256]{1,0:T(8,128)S(1)}, u32[]{:S(2)}, u32[]{:S(2)}) %collective-permute-start.12) | collective-permute-done | bytes 98336 | tf_op jit(solution)/shard_map/ppermute | solution.py:25
  137.5 8.1 %collective-permute-done.13.refs_11_ = f32[96,256]{1,0:T(8,128)S(1)} collective-permute-done((f32[96,256]{1,0:T(8,128)S(1)}, f32[96,256]{1,0:T(8,128)S(1)}, u32[]{:S(2)}, u32[]{:S(2)}) %collective-permute-start.13) | collective-permute-done | bytes 98336 | tf_op jit(solution)/shard_map/ppermute | solution.py:25
  145.7 0.5 shard_map.84
  146.2 8.7 %all_to_all.32 = f32[4,48,256]{2,1,0:T(8,128)S(1)} all-to-all(f32[4,48,256]{2,1,0:T(8,128)S(1)} %get-tuple-element.57), channel_id=1, replica_groups=mesh['y'=4,'z'=32,'core'=2,'grp'=4] {'grp'}, dimensions={0} | all-to-all | bytes 393216 | tf_op jit(solution)/shard_map/all_to_all | solution.py:37
  154.8 0.2 shard_map.86.refs_6_
  155.1 3.2 %collective-permute-start.16 = (f32[48,256]{1,0:T(8,128)S(1)}, f32[48,256]{1,0:T(8,128)S(1)}, u32[]{:S(2)}, u32[]{:S(2)}) collective-permute-start(f32[48,256]{1,0:T(8,128)S(1)} %shard_map.86.refs_6_), channel_id=1, source_target_pairs={{0,4},{4,8},{8,12},{12,16},{16,20},{20,24},{24,28},{28,32},{32,36}... | collective-permute-start | bytes 147464 | tf_op jit(solution)/shard_map/ppermute | solution.py:25
  158.3 4.2 %collective-permute-start.17 = (f32[48,256]{1,0:T(8,128)S(1)}, f32[48,256]{1,0:T(8,128)S(1)}, u32[]{:S(2)}, u32[]{:S(2)}) collective-permute-start(f32[48,256]{1,0:T(8,128)S(1)} %shard_map.86.refs_6_), channel_id=1, source_target_pairs={{4,0},{8,4},{12,8},{16,12},{20,16},{24,20},{28,24},{32,28},{36,32}... | collective-permute-start | bytes 147464 | tf_op jit(solution)/shard_map/ppermute | solution.py:25
  162.5 7.2 %collective-permute-start.18 = (f32[48,256]{1,0:T(8,128)S(1)}, f32[48,256]{1,0:T(8,128)S(1)}, u32[]{:S(2)}, u32[]{:S(2)}) collective-permute-start(f32[48,256]{1,0:T(8,128)S(1)} %shard_map.86.refs_6_), channel_id=1, source_target_pairs={{0,64},{4,68},{8,72},{12,76},{16,80},{20,84},{24,88},{28,92},{32,9... | collective-permute-start | bytes 147464 | tf_op jit(solution)/shard_map/ppermute | solution.py:25
  169.7 1.3 collective-permute-start.19
  171.0 1.6 shard_map.85
  172.7 0.3 shard_map.87
  173.0 0.0 collective-permute-done.18.refs_9_
  173.0 10.3 %collective-permute-done.19.refs_10_ = f32[48,256]{1,0:T(8,128)S(1)} collective-permute-done((f32[48,256]{1,0:T(8,128)S(1)}, f32[48,256]{1,0:T(8,128)S(1)}, u32[]{:S(2)}, u32[]{:S(2)}) %collective-permute-start.19) | collective-permute-done | bytes 49184 | tf_op jit(solution)/shard_map/ppermute | solution.py:25
  183.3 2.3 shard_map.88
  185.6 0.1 all_to_all.22
  185.7 24.2 %all_to_all.33 = f32[32,1,48]{2,1,0:T(1,128)S(1)} all-to-all(f32[32,1,48]{2,1,0:T(1,128)S(1)} %bitcast.33), channel_id=1, replica_groups=mesh['y'=4,'z'=32,'core'=2,'grp'=4] {'y','core','grp'}, dimensions={0} | all-to-all | bytes 12288 | tf_op jit(solution)/shard_map/all_to_all | solution.py:37
  209.9 0.1 reduce_sum.18
  210.0 35.4 %all_to_all.34 = f32[32,1,48]{2,1,0:T(1,128)S(1)} all-to-all(f32[32,1,48]{2,1,0:T(1,128)S(1)} %broadcast_in_dim.6), channel_id=1, replica_groups=mesh['y'=4,'z'=32,'core'=2,'grp'=4] {'z'}, dimensions={0} | all-to-all | bytes 12288 | tf_op jit(solution)/shard_map/all_to_all | solution.py:37
  245.4 12.0 %all_to_all.35 = f32[32,1,48]{2,1,0:T(1,128)S(1)} all-to-all(f32[32,1,48]{2,1,0:T(1,128)S(1)} %broadcast_in_dim.7), channel_id=1, replica_groups=mesh['y'=4,'z'=32,'core'=2,'grp'=4] {'y','core','grp'}, dimensions={0} | all-to-all | bytes 12288 | tf_op jit(solution)/shard_map/all_to_all | solution.py:37
  257.4 0.5 broadcast.9
  257.9 0.7 reduce.5
  258.6 0.1 reshape.34.refs_1_
  258.7 1.2 shard_map.89
  (15 shorter events, 0.1 us)
Async XLA Ops:
  2.8 26.7 %collective-permute-start = (f32[120,256]{1,0:T(8,128)}, f32[120,256]{1,0:T(8,128)S(1)}, u32[]{:S(2)}, u32[]{:S(2)}) collective-permute-start(f32[120,256]{1,0:T(8,128)} %get-tuple-element.36), channel_id=1, source_target_pairs={{0,4},{4,8},{8,12},{12,16},{16,20},{20,24},{24,28},{28,32},{32,36}... | collective-permute-start | bytes 368648 | tf_op jit(solution)/shard_map/ppermute | solution.py:25
  7.7 58.3 %collective-permute-start.4 = (f32[168,256]{1,0:T(8,128)}, f32[168,256]{1,0:T(8,128)S(1)}, u32[]{:S(2)}, u32[]{:S(2)}) collective-permute-start(f32[168,256]{1,0:T(8,128)} %get-tuple-element.40), channel_id=1, source_target_pairs={{0,1},{1,2},{2,3},{4,5},{5,6},{6,7},{8,9},{9,10},{10,11},{12,13},{... | collective-permute-start | bytes 516104 | tf_op jit(solution)/shard_map/ppermute | solution.py:25
  10.9 55.2 %collective-permute-start.5 = (f32[168,256]{1,0:T(8,128)}, f32[168,256]{1,0:T(8,128)S(1)}, u32[]{:S(2)}, u32[]{:S(2)}) collective-permute-start(f32[168,256]{1,0:T(8,128)} %get-tuple-element.41), channel_id=1, source_target_pairs={{1,0},{2,1},{3,2},{5,4},{6,5},{7,6},{9,8},{10,9},{11,10},{13,12},{... | collective-permute-start | bytes 516104 | tf_op jit(solution)/shard_map/ppermute | solution.py:25
  12.2 22.6 %collective-permute-start.1 = (f32[120,256]{1,0:T(8,128)}, f32[120,256]{1,0:T(8,128)S(1)}, u32[]{:S(2)}, u32[]{:S(2)}) collective-permute-start(f32[120,256]{1,0:T(8,128)} %get-tuple-element.37), channel_id=1, source_target_pairs={{4,0},{8,4},{12,8},{16,12},{20,16},{24,20},{28,24},{32,28},{36,32}... | collective-permute-start | bytes 368648 | tf_op jit(solution)/shard_map/ppermute | solution.py:25
  22.7 12.0 %collective-permute-start.2 = (f32[120,256]{1,0:T(8,128)}, f32[120,256]{1,0:T(8,128)S(1)}, u32[]{:S(2)}, u32[]{:S(2)}) collective-permute-start(f32[120,256]{1,0:T(8,128)} %get-tuple-element.38), channel_id=1, source_target_pairs={{0,64},{4,68},{8,72},{12,76},{16,80},{20,84},{24,88},{28,92},{32,9... | collective-permute-start | bytes 368648 | tf_op jit(solution)/shard_map/ppermute | solution.py:25
  29.6 36.5 %collective-permute-start.3 = (f32[120,256]{1,0:T(8,128)}, f32[120,256]{1,0:T(8,128)S(1)}, u32[]{:S(2)}, u32[]{:S(2)}) collective-permute-start(f32[120,256]{1,0:T(8,128)} %get-tuple-element.39), channel_id=1, source_target_pairs={{64,0},{68,4},{72,8},{76,12},{80,16},{84,20},{88,24},{92,28},{96,3... | collective-permute-start | bytes 368648 | tf_op jit(solution)/shard_map/ppermute | solution.py:25
  30.9 1.1 copy-start
  31.9 0.9 copy-start.2
  32.8 0.7 copy-start.4
  33.5 0.7 copy-start.5
  34.1 42.5 %copy-start.3 = (f32[1,1,48,192]{3,2,1,0:T(8,128)S(1)}, f32[1,1,48,192]{3,2,1,0:T(8,128)}, u32[]{:S(2)}) copy-start(f32[1,1,48,192]{3,2,1,0:T(8,128)} %param.9) | copy-start | bytes 110596
  66.6 42.1 %copy-start.1 = (f32[1,1,576,576]{3,2,1,0:T(8,128)S(1)}, f32[1,1,576,576]{3,2,1,0:T(8,128)}, u32[]{:S(2)}) copy-start(f32[1,1,576,576]{3,2,1,0:T(8,128)} %param.6) | copy-start | bytes 3981316
  76.8 20.8 %collective-permute-start.6 = (f32[48,256]{1,0:T(8,128)S(1)}, f32[48,256]{1,0:T(8,128)S(1)}, u32[]{:S(2)}, u32[]{:S(2)}) collective-permute-start(f32[48,256]{1,0:T(8,128)S(1)} %shard_map.80.refs_4_), channel_id=1, source_target_pairs={{0,4},{4,8},{8,12},{12,16},{16,20},{20,24},{24,28},{28,32},{32,36}... | collective-permute-start | bytes 147464 | tf_op jit(solution)/shard_map/ppermute | solution.py:25
  80.1 17.5 %collective-permute-start.7 = (f32[48,256]{1,0:T(8,128)S(1)}, f32[48,256]{1,0:T(8,128)S(1)}, u32[]{:S(2)}, u32[]{:S(2)}) collective-permute-start(f32[48,256]{1,0:T(8,128)S(1)} %shard_map.80.refs_4_), channel_id=1, source_target_pairs={{4,0},{8,4},{12,8},{16,12},{20,16},{24,20},{28,24},{32,28},{36,32}... | collective-permute-start | bytes 147464 | tf_op jit(solution)/shard_map/ppermute | solution.py:25
  82.4 15.3 %collective-permute-start.8 = (f32[48,256]{1,0:T(8,128)S(1)}, f32[48,256]{1,0:T(8,128)S(1)}, u32[]{:S(2)}, u32[]{:S(2)}) collective-permute-start(f32[48,256]{1,0:T(8,128)S(1)} %shard_map.80.refs_4_), channel_id=1, source_target_pairs={{0,64},{4,68},{8,72},{12,76},{16,80},{20,84},{24,88},{28,92},{32,9... | collective-permute-start | bytes 147464 | tf_op jit(solution)/shard_map/ppermute | solution.py:25
  95.1 13.6 %collective-permute-start.9 = (f32[48,256]{1,0:T(8,128)S(1)}, f32[48,256]{1,0:T(8,128)S(1)}, u32[]{:S(2)}, u32[]{:S(2)}) collective-permute-start(f32[48,256]{1,0:T(8,128)S(1)} %shard_map.80.refs_4_), channel_id=1, source_target_pairs={{64,0},{68,4},{72,8},{76,12},{80,16},{84,20},{88,24},{92,28},{96,3... | collective-permute-start | bytes 147464 | tf_op jit(solution)/shard_map/ppermute | solution.py:25
  111.2 18.0 %collective-permute-start.10 = (f32[96,256]{1,0:T(8,128)S(1)}, f32[96,256]{1,0:T(8,128)S(1)}, u32[]{:S(2)}, u32[]{:S(2)}) collective-permute-start(f32[96,256]{1,0:T(8,128)S(1)} %get-tuple-element.48.refs_3_), channel_id=1, source_target_pairs={{0,4},{4,8},{8,12},{12,16},{16,20},{20,24},{24,28},{28,32},{32,36}... | collective-permute-start | bytes 294920 | tf_op jit(solution)/shard_map/ppermute | solution.py:25
  114.8 15.7 %collective-permute-start.11 = (f32[96,256]{1,0:T(8,128)S(1)}, f32[96,256]{1,0:T(8,128)S(1)}, u32[]{:S(2)}, u32[]{:S(2)}) collective-permute-start(f32[96,256]{1,0:T(8,128)S(1)} %get-tuple-element.47.refs_2_), channel_id=1, source_target_pairs={{4,0},{8,4},{12,8},{16,12},{20,16},{24,20},{28,24},{32,28},{36,32}... | collective-permute-start | bytes 294920 | tf_op jit(solution)/shard_map/ppermute | solution.py:25
  118.8 11.7 %collective-permute-start.14 = (f32[96,256]{1,0:T(8,128)S(1)}, f32[96,256]{1,0:T(8,128)S(1)}, u32[]{:S(2)}, u32[]{:S(2)}) collective-permute-start(f32[96,256]{1,0:T(8,128)S(1)} %get-tuple-element.52.refs_7_), channel_id=1, source_target_pairs={{0,1},{1,2},{2,3},{4,5},{5,6},{6,7},{8,9},{9,10},{10,11},{12,13},{... | collective-permute-start | bytes 294920 | tf_op jit(solution)/shard_map/ppermute | solution.py:25
  121.0 9.5 %collective-permute-start.15 = (f32[96,256]{1,0:T(8,128)S(1)}, f32[96,256]{1,0:T(8,128)S(1)}, u32[]{:S(2)}, u32[]{:S(2)}) collective-permute-start(f32[96,256]{1,0:T(8,128)S(1)} %get-tuple-element.51.refs_6_), channel_id=1, source_target_pairs={{1,0},{2,1},{3,2},{5,4},{6,5},{7,6},{9,8},{10,9},{11,10},{13,12},{... | collective-permute-start | bytes 294920 | tf_op jit(solution)/shard_map/ppermute | solution.py:25
  122.3 15.3 %collective-permute-start.12 = (f32[96,256]{1,0:T(8,128)S(1)}, f32[96,256]{1,0:T(8,128)S(1)}, u32[]{:S(2)}, u32[]{:S(2)}) collective-permute-start(f32[96,256]{1,0:T(8,128)S(1)} %get-tuple-element.50.refs_5_), channel_id=1, source_target_pairs={{0,64},{4,68},{8,72},{12,76},{16,80},{20,84},{24,88},{28,92},{32,9... | collective-permute-start | bytes 294920 | tf_op jit(solution)/shard_map/ppermute | solution.py:25
  129.2 16.5 %collective-permute-start.13 = (f32[96,256]{1,0:T(8,128)S(1)}, f32[96,256]{1,0:T(8,128)S(1)}, u32[]{:S(2)}, u32[]{:S(2)}) collective-permute-start(f32[96,256]{1,0:T(8,128)S(1)} %get-tuple-element.49.refs_4_), channel_id=1, source_target_pairs={{64,0},{68,4},{72,8},{76,12},{80,16},{84,20},{88,24},{92,28},{96,3... | collective-permute-start | bytes 294920 | tf_op jit(solution)/shard_map/ppermute | solution.py:25
  155.1 17.9 %collective-permute-start.16 = (f32[48,256]{1,0:T(8,128)S(1)}, f32[48,256]{1,0:T(8,128)S(1)}, u32[]{:S(2)}, u32[]{:S(2)}) collective-permute-start(f32[48,256]{1,0:T(8,128)S(1)} %shard_map.86.refs_6_), channel_id=1, source_target_pairs={{0,4},{4,8},{8,12},{12,16},{16,20},{20,24},{24,28},{28,32},{32,36}... | collective-permute-start | bytes 147464 | tf_op jit(solution)/shard_map/ppermute | solution.py:25
  158.3 14.7 %collective-permute-start.17 = (f32[48,256]{1,0:T(8,128)S(1)}, f32[48,256]{1,0:T(8,128)S(1)}, u32[]{:S(2)}, u32[]{:S(2)}) collective-permute-start(f32[48,256]{1,0:T(8,128)S(1)} %shard_map.86.refs_6_), channel_id=1, source_target_pairs={{4,0},{8,4},{12,8},{16,12},{20,16},{24,20},{28,24},{32,28},{36,32}... | collective-permute-start | bytes 147464 | tf_op jit(solution)/shard_map/ppermute | solution.py:25
  162.5 10.5 %collective-permute-start.18 = (f32[48,256]{1,0:T(8,128)S(1)}, f32[48,256]{1,0:T(8,128)S(1)}, u32[]{:S(2)}, u32[]{:S(2)}) collective-permute-start(f32[48,256]{1,0:T(8,128)S(1)} %shard_map.86.refs_6_), channel_id=1, source_target_pairs={{0,64},{4,68},{8,72},{12,76},{16,80},{20,84},{24,88},{28,92},{32,9... | collective-permute-start | bytes 147464 | tf_op jit(solution)/shard_map/ppermute | solution.py:25
  169.7 13.5 %collective-permute-start.19 = (f32[48,256]{1,0:T(8,128)S(1)}, f32[48,256]{1,0:T(8,128)S(1)}, u32[]{:S(2)}, u32[]{:S(2)}) collective-permute-start(f32[48,256]{1,0:T(8,128)S(1)} %shard_map.86.refs_6_), channel_id=1, source_target_pairs={{64,0},{68,4},{72,8},{76,12},{80,16},{84,20},{88,24},{92,28},{96,3... | collective-permute-start | bytes 147464 | tf_op jit(solution)/shard_map/ppermute | solution.py:25
